TPU v7x, 32 devices: a whole 2x2x4 slice. The times are simulated.
32 devices in a mesh: wide: 8 (over z, x), narrow: 4 (over y, core).
Axes of the slice: x: 2, y: 2, z: 4, core: 2. Of those that a mesh axis runs over, the one named last changes fastest.
Arguments:
- hidden_in: bfloat16 [16384, 1024], P(('wide', 'narrow')), may hold values from -6 to 6
- grad_out: bfloat16 [16384, 1024], P(('wide', 'narrow')), may hold values from -6 to 6
- gain_attn: bfloat16 [1024], replicated, may hold values from 0.5 to 1.5
- gain_ffn: bfloat16 [1024], replicated, may hold values from 0.5 to 1.5
- w_query: bfloat16 [1024, 1024], P(None, 'narrow'), may hold values from -0.046875 to 0.046875
- w_key: bfloat16 [1024, 1024], P(None, 'narrow'), may hold values from -0.1875 to 0.1875
- w_value: bfloat16 [1024, 1024], P(None, 'narrow'), may hold values from -0.1875 to 0.1875
- w_output: bfloat16 [1024, 1024], P('narrow'), may hold values from -0.75 to 0.75
- table_rel: bfloat16 [32, 16], P(None, 'narrow'), may hold values from -4 to 4
- table_horiz: bfloat16 [32, 16], P(None, 'narrow'), may hold values from -4 to 4
- table_vert: bfloat16 [32, 16], P(None, 'narrow'), may hold values from -4 to 4
- wi_gate: bfloat16 [1024, 2816], P(None, 'narrow'), may hold values from -0.1875 to 0.1875
- wi_up: bfloat16 [1024, 2816], P(None, 'narrow'), may hold values from -0.1875 to 0.1875
- wo_ffn: bfloat16 [2816, 1024], P('narrow'), may hold values from -0.21875 to 0.21875
- counts: int32 [32], P('wide'), may hold values from 1 to 256
- patch_mask: int32 [32, 256], P('wide'), may hold values 0 or 1
- bucket_rel: int32 [32, 512, 512], P('wide'), may hold values from 0 to 31
- bucket_horiz: int32 [32, 512, 512], P('wide'), may hold values from 0 to 31
- bucket_vert: int32 [32, 512, 512], P('wide'), may hold values from 0 to 31
Outputs:
- block_out: bfloat16 [16384, 1024], P(('wide', 'narrow'))
- grad_input: float32 [16384, 1024], P(('wide', 'narrow'))
- grad_gain_attn: float32 [1024], P(('wide', 'narrow'))
- grad_gain_ffn: float32 [1024], P(('wide', 'narrow'))
- grad_w_query: float32 [1024, 1024], P('wide', 'narrow')
- grad_w_key: float32 [1024, 1024], P('wide', 'narrow')
- grad_w_value: float32 [1024, 1024], P('wide', 'narrow')
- grad_w_output: float32 [1024, 1024], P('narrow', 'wide')
- grad_table_rel: float32 [32, 16], P('wide', 'narrow')
- grad_table_horiz: float32 [32, 16], P('wide', 'narrow')
- grad_table_vert: float32 [32, 16], P('wide', 'narrow')
- grad_wi_gate: float32 [1024, 2816], P('wide', 'narrow')
- grad_wi_up: float32 [1024, 2816], P('wide', 'narrow')
- grad_wo_ffn: float32 [2816, 1024], P('narrow', 'wide')
All inputs are finite; a program needn't handle non-finite values. No bound on the sum of `patch_mask` on one device may be relied on, other than what follows from the above.
Results may differ from a plain program's by a relative error of at most 0.02.
Values may be sent and summed in bfloat16 or wider, within the bound.
A program may use at most 256 MiB of HBM per device.

v0:
```python
import functools
import math

import jax
import jax.numpy as jnp
from jax import lax
from jax.experimental import pallas as pl
from jax.experimental.pallas import tpu as pltpu
from jax.sharding import PartitionSpec as P

F32 = jnp.float32
BF = jnp.bfloat16
I32 = jnp.int32
HEAD_DIM = 64
LANES = 128
EPS = 1e-06
NT = (((1,), (1,)), ((), ()))

FIXED = 2048.0
OFFSET = 8192
MASKED = -3.0e12
VMEM_LIMIT = 60 << 20
MESH = pl.DeviceIdType.MESH


def lookup(table_row, ids):
    return jnp.take_along_axis(table_row, ids, axis=1, mode="promise_in_bounds")


def neighbours():
    w, n = lax.axis_index("wide"), lax.axis_index("narrow")
    return w, n, (w, n ^ 1), (w, n ^ 2), (w, n ^ 3), (w ^ 1, n)


def greet(devices):
    barrier = pltpu.get_barrier_semaphore()
    for device in devices:
        pl.semaphore_signal(barrier, inc=1, device_id=device, device_id_type=MESH)
    pl.semaphore_wait(barrier, len(devices))


def remote(src, dst, sems, device):
    return pltpu.make_async_remote_copy(
        src_ref=src, dst_ref=dst, send_sem=sems.at[0], recv_sem=sems.at[1], device_id=device, device_id_type=MESH
    )


def forward_kernel(
    heads, chunk,
    x_ref, gain1_ref, gain2_ref, valid_ref, tab_ref, wq_ref, wk_ref, wv_ref, wo_ref, ir_ref, ih_ref, iv_ref,
    go_ref, wg_ref, wu_ref, wd_ref,
    qkv_ref, e_ref, ctx_ref, linv_ref, wall_ref, woall_ref, middle_ref, ffn_ref, gofar_ref, wgc_ref, wuc_ref, wdc_ref,
    normed_ref, mask_ref, ids_ref, tabs_ref, words_ref, ebuf_ref,
    own_sem, id_sem, e_sem, core_sem, far_sem, wide_sem, fwd_sem, tab_sem, big_sem,
):
    pw = 2 * HEAD_DIM
    slots, d = x_ref.shape
    w, n, core, far, diag, side = neighbours()
    half = w & 1
    other = 1 - half

    def source(m, pair):
        cols = pl.ds(pl.multiple_of(pair * pw, pw), pw)
        return wo_ref.at[cols, :] if m == 3 else (wq_ref, wk_ref, wv_ref)[m].at[:, cols]

    def place(m, slot):
        cols = pl.ds(pl.multiple_of(slot * pw, pw), pw)
        return woall_ref.at[cols, :] if m == 3 else wall_ref.at[m, :, cols]

    ids_in = [pltpu.make_async_copy(r.at[n], ids_ref.at[t], id_sem.at[t]) for t, r in enumerate((ir_ref, ih_ref, iv_ref))]
    own_in = [[pltpu.make_async_copy(source(m, p), place(m, p), own_sem.at[p, m]) for m in range(4)] for p in range(2)]
    for copy in own_in[0][:3] + ids_in + own_in[0][3:] + own_in[1]:
        copy.start()

    greet((core, far, diag, side))
    far_out = [remote(source(m, half), place(m, 4 + half), far_sem.at[m], far) for m in range(4)]
    core_out = [[remote(source(m, p), place(m, 2 + p), core_sem.at[p, m], core) for m in range(4)] for p in range(2)]
    tabs_out = [remote(tab_ref, tabs_ref.at[r], tab_sem.at[r - 1], dev) for r, dev in ((1, core), (2, far), (3, diag))]
    for copy in tabs_out + far_out[:1] + core_out[0] + core_out[1] + far_out[1:]:
        copy.start()
    wide_out = [remote(place(m, 4 + half), place(m, 4 + half), wide_sem.at[m], side) for m in range(4)]
    fwd_out = [
        [remote(place(m, 4 + p), place(m, 6 + p), fwd_sem.at[i, m], core) for m in range(4)]
        for i, p in enumerate((half, other))
    ]
    go_out = remote(go_ref, gofar_ref, big_sem.at[0], far)
    ffn_out = [
        remote(wg_ref, wgc_ref, big_sem.at[1], core),
        remote(wu_ref, wuc_ref, big_sem.at[2], core),
        remote(wd_ref, wdc_ref, big_sem.at[3], core),
    ]

    x = x_ref[...].astype(F32)
    inv = lax.rsqrt(jnp.mean(x * x, axis=-1, keepdims=True) + EPS)
    normed_ref[...] = (x * inv * gain1_ref[...]).astype(BF)
    lane_all = lax.broadcasted_iota(I32, (slots, pw), 1)
    shown = jnp.broadcast_to(valid_ref[...], (slots, pw)) > 0.5
    mask_ref[...] = jnp.where(lane_all == 0, jnp.where(shown, 0.0, MASKED), 0.0).astype(BF)
    ones = jnp.ones((slots, pw), BF)
    lane = lax.broadcasted_iota(I32, (chunk, pw), 1)
    low = lane < HEAD_DIM
    first = jnp.where(lane == 0, 1.0, 0.0).astype(BF)
    to_log2 = math.log2(math.e) / FIXED

    tabs_ref[0] = tab_ref[...]
    for copy in ids_in:
        copy.wait()
    for copy in tabs_out:
        copy.wait()
    for r in range(4):
        fixed = tabs_ref[r].astype(I32)
        for p in range(2):
            for t in range(3):
                row = t * heads + 2 * p
                words_ref[2 * r + p, t : t + 1, :] = fixed[row + 1 : row + 2] * 65536 + fixed[row : row + 1] + OFFSET

    def e_out(parity, slot):
        return pltpu.make_async_copy(ebuf_ref.at[parity], e_ref.at[slot], e_sem.at[parity])

    def slot_of(t):
        late = 4 + 2 * (t & 1) + jnp.where(t >= 6, other, half)
        return jnp.where(t < 4, t, late)

    def step(t, carry):
        slot = slot_of(t)
        for p in range(2):

            @pl.when(t == p)
            def _():
                for m in range(3):
                    own_in[p][m].wait()

            @pl.when(t == 2 + p)
            def _():
                for m in range(3):
                    core_out[p][m].wait_recv()

        for m in range(4):

            @pl.when(t == 2 + m)
            def _():
                far_out[m].wait_recv()
                wide_out[m].start()
                fwd_out[0][m].start()

        @pl.when(t == 3)
        def _():
            for copy in ffn_out:
                copy.start()

        @pl.when(t == 4)
        def _():
            go_out.start()

        @pl.when(t == 5)
        def _():
            for m in range(3):
                fwd_out[0][m].wait_recv()

        @pl.when(t == 6)
        def _():
            for m in range(3):
                wide_out[m].wait_recv()
                fwd_out[1][m].start()

        @pl.when(t == 7)
        def _():
            for m in range(3):
                fwd_out[1][m].wait_recv()
            wide_out[3].wait_recv()
            fwd_out[1][3].start()

        parity = t & 1

        @pl.when(t >= 2)
        def _():
            e_out(parity, slot).wait()

        cols = pl.ds(pl.multiple_of(slot * pw, pw), pw)
        weights = jnp.concatenate([wall_ref[m, :, cols] for m in range(3)], axis=1)
        joined = jnp.dot(normed_ref[...], weights, preferred_element_type=F32).astype(BF)
        for m in range(3):
            qkv_ref[m, :, cols] = joined[:, m * pw : (m + 1) * pw]
        kx = jnp.concatenate([joined[:, pw : 2 * pw], mask_ref[...]], axis=1)
        vx = jnp.concatenate([joined[:, 2 * pw :], ones], axis=1)
        words = words_ref[slot]
        for c in range(slots // chunk):
            rows = slice(c * chunk, (c + 1) * chunk)
            q2 = joined[rows, :pw] * jnp.bfloat16(FIXED)
            zero = jnp.zeros_like(q2)
            scores = []
            for sub in range(2):
                q = jnp.where(low, q2, zero) if sub == 0 else jnp.where(low, zero, q2)
                q = jnp.concatenate([q, first], axis=1)
                scores.append(lax.dot_general(q, kx, NT, preferred_element_type=F32))
            tabs = [jnp.broadcast_to(words[k : k + 1, :], (chunk, LANES)) for k in range(3)]
            parts = ([], [])
            for j in range(slots // LANES):
                sl = slice(j * LANES, (j + 1) * LANES)
                bias = (
                    lookup(tabs[0], ids_ref[0, rows, sl])
                    + lookup(tabs[1], ids_ref[1, rows, sl])
                    + lookup(tabs[2], ids_ref[2, rows, sl])
                )
                parts[0].append(scores[0][:, sl] + (bias & 0xFFFF).astype(F32))
                parts[1].append(scores[1][:, sl] + (bias >> 16).astype(F32))
            outs = []
            for sub in range(2):
                s = jnp.concatenate(parts[sub], axis=1)
                peak = jnp.max(s, axis=1, keepdims=True)
                e = jnp.exp2((s - peak) * to_log2).astype(BF)
                ebuf_ref[parity, sub, rows, :] = e
                outs.append(jnp.dot(e, vx, preferred_element_type=F32))
            linv = 1.0 / jnp.where(low, outs[0][:, pw:], outs[1][:, pw:])
            linv_ref[rows, cols] = linv
            ctx_ref[rows, cols] = (jnp.where(low, outs[0][:, :pw], outs[1][:, :pw]) * linv).astype(BF)
        e_out(parity, slot).start()
        return carry

    lax.fori_loop(0, 8, step, 0)
    for p in range(2):
        own_in[p][3].wait()
        core_out[p][3].wait_recv()
    for i in range(2):
        fwd_out[i][3].wait_recv()
    middle = x_ref[...].astype(F32) + jnp.dot(ctx_ref[...], woall_ref[...], preferred_element_type=F32)
    middle_ref[...] = middle
    inv = lax.rsqrt(jnp.mean(middle * middle, axis=-1, keepdims=True) + EPS)
    ffn_ref[...] = (middle * inv * gain2_ref[...]).astype(BF)
    for p in range(2):
        e_out(p, p).wait()
        for m in range(4):
            core_out[p][m].wait_send()
            fwd_out[p][m].wait_send()
    for m in range(4):
        far_out[m].wait_send()
        wide_out[m].wait_send()
    for copy in ffn_out:
        copy.wait()
    go_out.wait()


def forward(x, gain1, gain2, valid, tab, wq, wk, wv, wo, ids, grad_out, wg, wu, wd, chunk=256):
    slots, d = x.shape
    heads = wq.shape[1] // HEAD_DIM
    ff = wd.shape[0]
    assert heads == 4
    vmem, anywhere = pl.BlockSpec(memory_space=pltpu.VMEM), pl.BlockSpec(memory_space=pl.ANY)
    shape = jax.ShapeDtypeStruct
    dma = pltpu.SemaphoreType.DMA
    return pl.pallas_call(
        functools.partial(forward_kernel, heads, chunk),
        in_specs=[vmem] * 5 + [anywhere] * 11,
        out_specs=[vmem, anywhere] + [vmem] * 6 + [anywhere] * 4,
        out_shape=[
            shape((3, slots, d), BF),
            shape((8, 2, slots, slots), BF),
            shape((slots, d), BF),
            shape((slots, d), F32),
            shape((3, d, d), BF),
            shape((d, d), BF),
            shape((slots, d), F32),
            shape((slots, d), BF),
            shape((slots, d), BF),
            shape((ff, d), BF),
            shape((ff, d), BF),
            shape((ff, d), BF),
        ],
        scratch_shapes=[
            pltpu.VMEM((slots, d), BF),
            pltpu.VMEM((slots, 2 * HEAD_DIM), BF),
            pltpu.VMEM((3, slots, slots), I32),
            pltpu.VMEM((4, 16, LANES), F32),
            pltpu.VMEM((8, 8, LANES), I32),
            pltpu.VMEM((2, 2, slots, slots), BF),
            dma((2, 4)), dma((3,)), dma((2,)), dma((2, 4, 2)), dma((4, 2)), dma((4, 2)), dma((2, 4, 2)),
            dma((3, 2)), dma((4, 2)),
        ],
        compiler_params=pltpu.CompilerParams(
            vmem_limit_bytes=VMEM_LIMIT, collective_id=1, has_side_effects=True
        ),
        cost_estimate=pl.CostEstimate(flops=20 * slots * d * d, bytes_accessed=40 << 20, transcendentals=16 * slots * slots),
        name="forward",
    )(x, gain1, gain2, valid, tab, wq, wk, wv, wo, *ids, grad_out, wg, wu, wd)


def gelu_parts(v):
    c, k = math.sqrt(2.0 / math.pi), 0.044715
    square = v * v
    t = jnp.tanh(c * v * (1.0 + k * square))
    up = 0.5 * (1.0 + t)
    slope = up + 0.5 * v * (1.0 - t * t) * (c * (1.0 + 3.0 * k * square))
    return v * up, slope


def ffn_kernel(
    block,
    x_ref, go_ref, gofar_ref, middle_ref, gain_ref, w0_ref, w1_ref, w2_ref, c0_ref, c1_ref, c2_ref,
    out_ref, sum_ref, gm_ref, ga_ref, gain_out_ref,
    xall_ref, gall_ref, w_ref, xt_ref, gt_ref, act_ref, send_ref, recv_ref, own_ref, backfar_ref, backin_ref,
    in_sem, w_sem, x_sem, back_sem, dw_sem,
):
    slots, d = middle_ref.shape
    ff = w_ref.shape[2]
    halves = slots // block
    _, _, core, far, _, _ = neighbours()

    ins = [
        pltpu.make_async_copy(x_ref, xall_ref.at[pl.ds(0, slots), :], in_sem.at[0]),
        pltpu.make_async_copy(go_ref, gall_ref.at[pl.ds(0, slots), :], in_sem.at[1]),
        pltpu.make_async_copy(gofar_ref, gall_ref.at[pl.ds(slots, slots), :], in_sem.at[2]),
    ]
    weights = [
        [pltpu.make_async_copy(r, w_ref.at[q, m], w_sem.at[q, m]) for m, r in enumerate(group)]
        for q, group in enumerate(((w0_ref, w1_ref, w2_ref), (c0_ref, c1_ref, c2_ref)))
    ]
    for copy in ins[:2] + weights[0] + weights[1] + ins[2:]:
        copy.start()
    greet((core, far))
    x_out = [
        remote(x_ref.at[pl.ds(i * block, block), :], xall_ref.at[pl.ds(slots + i * block, block), :], x_sem.at[i], far)
        for i in range(halves)
    ]
    for copy in x_out:
        copy.start()
    back_out = [
        remote(backfar_ref.at[pl.ds(i * block, block), :], backin_ref.at[pl.ds(i * block, block), :], back_sem.at[i], far)
        for i in range(halves)
    ]
    for copy in ins + weights[0] + weights[1]:
        copy.wait()

    def step(b, carry):
        for i in range(halves):

            @pl.when(b == halves + i)
            def _():
                x_out[i].wait_recv()

        rows = pl.ds(pl.multiple_of(b * block, block), block)
        x, g = xall_ref[rows, :], gall_ref[rows, :]
        xt_ref[:, rows] = x.T
        gt_ref[:, rows] = g.T
        out = back = None
        for q in range(2):
            gate = lax.dot_general(x, w_ref[q, 0], NT, preferred_element_type=F32)
            upper = lax.dot_general(x, w_ref[q, 1], NT, preferred_element_type=F32)
            grad_hidden = lax.dot_general(g, w_ref[q, 2], NT, preferred_element_type=F32)
            gelu, slope = gelu_parts(gate)
            dg = (grad_hidden * upper * slope).astype(BF)
            du = (grad_hidden * gelu).astype(BF)
            hidden = (gelu * upper).astype(BF)
            act_ref[q, 0, rows, :] = dg
            act_ref[q, 1, rows, :] = du
            act_ref[q, 2, rows, :] = hidden
            o = jnp.dot(hidden, w_ref[q, 2], preferred_element_type=F32)
            k = jnp.dot(dg, w_ref[q, 0], preferred_element_type=F32)
            k = k + jnp.dot(du, w_ref[q, 1], preferred_element_type=F32)
            out, back = (o, k) if q == 0 else (out + o, back + k)
        out_ref[rows, :] = out.astype(BF)

        @pl.when(b < halves)
        def _():
            own_ref[rows, :] = back

        for i in range(halves):

            @pl.when(b == halves + i)
            def _():
                backfar_ref[i * block : (i + 1) * block, :] = back.astype(BF)
                back_out[i].start()

        return carry

    lax.fori_loop(0, 2 * halves, step, 0)

    tile = 256
    dw_out = [remote(send_ref.at[m], recv_ref.at[m], dw_sem.at[m], core) for m in range(3)]
    for q in (1, 0):
        for m in range(3):
            left = gt_ref if m == 2 else xt_ref
            target = send_ref if q == 1 else sum_ref

            def part(c, carry):
                rows = pl.ds(pl.multiple_of(c * tile, tile), tile)
                target[m, rows, :] = jnp.dot(left[rows, :], act_ref[q, m], preferred_element_type=F32).astype(BF)
                return carry

            lax.fori_loop(0, d // tile, part, 0)
            if q == 1:
                dw_out[m].start()
    for m in range(3):
        dw_out[m].wait_recv()
        sum_ref[m] = (sum_ref[m].astype(F32) + recv_ref[m].astype(F32)).astype(BF)

    for copy in back_out:
        copy.wait_recv()
    middle = middle_ref[...]
    inv = lax.rsqrt(jnp.mean(middle * middle, axis=-1, keepdims=True) + EPS)
    upstream = own_ref[...] + backin_ref[...].astype(F32)
    lifted = upstream * gain_ref[...]
    inner = jnp.mean(lifted * middle, axis=-1, keepdims=True)
    gain_out_ref[...] = jnp.sum(upstream * middle * inv, axis=0, keepdims=True)
    gm = gall_ref[0:slots, :].astype(F32) + inv * lifted - middle * (inv * inv * inv * inner)
    gm_ref[...] = gm
    ga_ref[...] = gm.astype(BF)
    for copy in x_out + back_out + dw_out:
        copy.wait_send()


def feed_forward(x, go, gofar, middle, gain, own, other, block=256):
    slots, d = x.shape
    ff = own[0].shape[0]
    vmem, anywhere = pl.BlockSpec(memory_space=pltpu.VMEM), pl.BlockSpec(memory_space=pl.ANY)
    shape = jax.ShapeDtypeStruct
    dma = pltpu.SemaphoreType.DMA
    halves = slots // block
    return pl.pallas_call(
        functools.partial(ffn_kernel, block),
        in_specs=[anywhere] * 3 + [vmem] * 2 + [anywhere] * 6,
        out_specs=[vmem] * 5,
        out_shape=[
            shape((2 * slots, d), BF),
            shape((3, d, ff), BF),
            shape((slots, d), F32),
            shape((slots, d), BF),
            shape((1, d), F32),
        ],
        scratch_shapes=[
            pltpu.VMEM((2 * slots, d), BF),
            pltpu.VMEM((2 * slots, d), BF),
            pltpu.VMEM((2, 3, ff, d), BF),
            pltpu.VMEM((d, 2 * slots), BF),
            pltpu.VMEM((d, 2 * slots), BF),
            pltpu.VMEM((2, 3, 2 * slots, ff), BF),
            pltpu.VMEM((3, d, ff), BF),
            pltpu.VMEM((3, d, ff), BF),
            pltpu.VMEM((slots, d), F32),
            pltpu.VMEM((slots, d), BF),
            pltpu.VMEM((slots, d), BF),
            dma((3,)), dma((2, 3)), dma((halves, 2)), dma((halves, 2)), dma((3, 2)),
        ],
        compiler_params=pltpu.CompilerParams(
            vmem_limit_bytes=VMEM_LIMIT, collective_id=2, has_side_effects=True
        ),
        cost_estimate=pl.CostEstimate(flops=36 * slots * d * ff, bytes_accessed=40 << 20, transcendentals=4 * slots * ff),
        name="feed_forward",
    )(x, go, gofar, middle, gain, *own, *other)


def backward_kernel(
    wide, heads, buckets, trows,
    ga_ref, x_ref, gain_ref, gain2_ref, fsum_ref, gm_ref, e_ref, ir_ref, ih_ref, iv_ref, out_ref,
    wo_ref, ctx_ref, linv_ref, qkv_ref, wall_ref,
    gi_ref, outin_ref, small_ref, gq_ref, gk_ref, gv_ref, go_ref, fg_ref, fu_ref, fd_ref,
    ds_ref, ids_ref, nt_ref, gat_ref, dx_ref, acc_ref, part_ref, crecv_ref, frecv_ref, xarecv_ref, zarecv_ref,
    xfrecv_ref, zfrecv_ref, nsend_ref, nrecv_ref, sxrecv_ref, szrecv_ref,
    in_sem, e_sem, core_sem, far_sem, out_sem, xf_sem, zf_sem, xa_sem, za_sem, sn_sem, sx_sem, sz_sem,
):
    pw = 2 * HEAD_DIM
    slots, d = ga_ref.shape
    half_rows = slots // 2
    ranks = wide // 2
    chunk = d // wide
    steps = 8 + slots // trows
    u = pl.program_id(0)
    w, n, core, far, diag, side = neighbours()
    par, rank = w & 1, w >> 1
    opp = 1 - par
    peer = lambda r: (2 * (rank ^ r) + par, n)
    slot_of = lambda k: 6 - 2 * (k >> 1) + (k & 1)
    slot = slot_of(jnp.minimum(u, 7))

    ins = [pltpu.make_async_copy(r.at[n], ids_ref.at[t], in_sem.at[t]) for t, r in enumerate((ir_ref, ih_ref, iv_ref))]
    gm_in = pltpu.make_async_copy(gm_ref, gi_ref, in_sem.at[3])
    core_out = [remote(part_ref.at[s], crecv_ref.at[i], core_sem.at[i], core) for i, s in enumerate((6, 7, 2, 3))]
    far_out = [
        [remote(part_ref.at[4 + i, :, p], frecv_ref.at[i, :, p], far_sem.at[i, k], far) for k, p in enumerate((opp, par))]
        for i in range(2)
    ]
    out_out = [
        remote(
            out_ref.at[pl.ds(slots + i * half_rows, half_rows), :],
            outin_ref.at[pl.ds(i * half_rows, half_rows), :], out_sem.at[i], far,
        )
        for i in range(2)
    ]
    xf_out = [remote(fsum_ref.at[:, rank ^ r, opp], xfrecv_ref.at[r], xf_sem.at[r], side) for r in range(ranks)]
    zf_out = [None] + [remote(xfrecv_ref.at[r], zfrecv_ref.at[r - 1], zf_sem.at[r - 1], peer(r)) for r in range(1, ranks)]
    xa_out = [remote(part_ref.at[i, :, opp], xarecv_ref.at[i], xa_sem.at[i], side) for i in range(2)]
    za_out = [
        [None]
        + [remote(part_ref.at[i, rank ^ r, par], zarecv_ref.at[i, r - 1], za_sem.at[i, r - 1], peer(r)) for r in range(1, ranks)]
        for i in range(2)
    ]
    sn_out = [
        remote(nsend_ref.at[r], nrecv_ref.at[r - 1], sn_sem.at[r - 1], dev) for r, dev in ((1, core), (2, far), (3, diag))
    ]
    sx_out = remote(nsend_ref.at[1], sxrecv_ref, sx_sem, side)
    sz_out = [None] + [remote(nsend_ref.at[2], szrecv_ref.at[r - 1], sz_sem.at[r - 1], peer(r)) for r in range(1, ranks)]

    def e_in(k):
        s = slot_of(k)
        return pltpu.make_async_copy(e_ref.at[s], ds_ref.at[s], e_sem.at[k & 1])

    def wide_f32(ref_value):
        return ref_value.astype(F32)

    @pl.when(u == 0)
    def _():
        e_in(0).start()
        for copy in ins + [gm_in]:
            copy.start()
        greet([core, far, diag, side] + [peer(r) for r in range(1, ranks)])
        for r in range(1, max(2, ranks - 1)):
            xf_out[r].start()
        out_out[0].start()
        x = x_ref[...].astype(F32)
        inv = lax.rsqrt(jnp.mean(x * x, axis=-1, keepdims=True) + EPS)
        nt_ref[...] = (x * inv * gain_ref[...]).astype(BF).T
        gat_ref[...] = ga_ref[...].T
        dx_ref[...] = jnp.zeros_like(dx_ref)
        acc_ref[...] = jnp.zeros_like(acc_ref)

    @pl.when(u < 8)
    def _():
        e_in(u).wait()

        @pl.when(u < 7)
        def _():
            e_in(u + 1).start()

        lane = lax.broadcasted_iota(I32, (slots, pw), 1)
        low = lane < HEAD_DIM
        do2 = (lax.dot_general(ga_ref[...], wo_ref[...], NT, preferred_element_type=F32) * linv_ref[...]).astype(BF)
        prod = do2.astype(F32) * ctx_ref[...].astype(F32)
        q2, k2, v2 = qkv_ref[0], qkv_ref[1], qkv_ref[2]
        vx = jnp.concatenate([v2, jnp.where(lane < 2, 1.0, 0.0).astype(BF)], axis=1)
        do_t, q_t = do2.T, q2.T
        zero = jnp.zeros_like(do2)
        dq, dk, dv = [], [], []
        for sub in range(2):
            mine = low if sub == 0 else jnp.logical_not(low)
            row = -jnp.sum(jnp.where(mine, prod, 0.0), axis=1, keepdims=True)
            head_part = row.astype(BF).astype(F32)
            extra = jnp.where(lane == 0, head_part, jnp.where(lane == 1, row - head_part, 0.0)).astype(BF)
            dox = jnp.concatenate([jnp.where(mine, do2, zero), extra], axis=1)
            t = lax.dot_general(dox, vx, NT, preferred_element_type=F32)
            e = ds_ref[slot, sub]
            ds = (e.astype(F32) * t).astype(BF)
            dv.append(jnp.dot(do_t[sub * HEAD_DIM : (sub + 1) * HEAD_DIM], e, preferred_element_type=F32))
            ds_ref[slot, sub] = ds
            dk.append(jnp.dot(q_t[sub * HEAD_DIM : (sub + 1) * HEAD_DIM], ds, preferred_element_type=F32))
            dq.append(jnp.dot(ds, k2, preferred_element_type=F32))
        joined = jnp.concatenate(
            [
                jnp.where(low, dq[0], dq[1]).astype(BF),
                jnp.concatenate(dk, axis=0).T.astype(BF),
                jnp.concatenate(dv, axis=0).T.astype(BF),
            ],
            axis=1,
        )
        weights = jnp.concatenate([wall_ref[m] for m in range(3)], axis=1)
        dx_ref[...] += lax.dot_general(joined, weights, NT, preferred_element_type=F32)
        part = jnp.dot(nt_ref[...], joined, preferred_element_type=F32).astype(BF)
        part_ref[slot, :, :, :, : 3 * pw] = part.reshape(ranks, 2, chunk, 3 * pw)
        part = jnp.dot(gat_ref[...], ctx_ref[...], preferred_element_type=F32).astype(BF)
        part_ref[slot, :, :, :, 3 * pw :] = part.reshape(ranks, 2, chunk, pw)

    @pl.when(u >= 8)
    def _():
        blk = 16
        one, zero = jnp.ones((blk, slots), BF), jnp.zeros((blk, slots), BF)

        @pl.when(u == 8)
        def _():
            for copy in ins:
                copy.wait()

        def sub_block(c, carry):
            rows = pl.ds(pl.multiple_of((u - 8) * trows + c * blk, blk), blk)
            g = jnp.concatenate([ds_ref[s, sub, rows, :] for s in range(8) for sub in range(2)], axis=0)
            for t in range(3):
                ids = ids_ref[t, rows, :].astype(F32).astype(BF)
                hot = jnp.concatenate([jnp.where(ids == jnp.bfloat16(b), one, zero) for b in range(buckets)], axis=0)
                span = slice(t * buckets * blk, (t + 1) * buckets * blk)
                acc_ref[span, :] += lax.dot_general(hot, g, NT, preferred_element_type=F32)
            return carry

        lax.fori_loop(0, trows // blk, sub_block, 0)

    def event(step):
        return lambda body: pl.when(u == step)(body)

    for i in range(2):

        @event(i)
        def _():
            core_out[i].start()

        @event(4 + i)
        def _():
            core_out[2 + i].start()

        @event(2 + i)
        def _():
            core_out[i].wait_recv()
            for k, p in enumerate((opp, par)):
                total = wide_f32(part_ref[4 + i, :, p]) + wide_f32(crecv_ref[i, :, p])
                part_ref[4 + i, :, p] = total.astype(BF)
                far_out[i][k].start()

    def far_stage(i):
        core_out[2 + i].wait_recv()
        far_out[i][0].wait_recv()
        total = wide_f32(part_ref[i, :, opp]) + wide_f32(crecv_ref[2 + i, :, opp]) + wide_f32(frecv_ref[i, :, opp])
        part_ref[i, :, opp] = total.astype(BF)
        xa_out[i].start()

    def side_stage(i):
        far_out[i][1].wait_recv()
        xa_out[i].wait_recv()
        total = wide_f32(part_ref[i, :, par]) + wide_f32(crecv_ref[2 + i, :, par])
        total = total + wide_f32(frecv_ref[i, :, par]) + wide_f32(xarecv_ref[i])
        part_ref[i, :, par] = total.astype(BF)
        for r in range(1, ranks):
            za_out[i][r].start()

    def ffn_stage(r):
        xf_out[r].wait_recv()
        xfrecv_ref[r] = (wide_f32(fsum_ref[:, rank ^ r, par]) + wide_f32(xfrecv_ref[r])).astype(BF)
        if r > 0:
            zf_out[r].start()

    for r in range(1, ranks):

        @event(3 + (r - 1) * 6 // max(1, ranks - 2))
        def _():
            ffn_stage(r)

    @event(4)
    def _():
        if ranks > 2:
            xf_out[ranks - 1].start()

    event(6)(lambda: far_stage(0))

    @event(7)
    def _():
        gm_in.wait()
        x = x_ref[...].astype(F32)
        inv = lax.rsqrt(jnp.mean(x * x, axis=-1, keepdims=True) + EPS)
        upstream = dx_ref[...]
        lifted = upstream * gain_ref[...]
        inner = jnp.mean(lifted * x, axis=-1, keepdims=True)
        gi_ref[...] = gi_ref[...] + inv * lifted - x * (inv * inv * inv * inner)
        gains = jnp.sum(upstream * x * inv, axis=0, keepdims=True)
        lanes = d // LANES
        for r in range(4):
            for j in range(lanes):
                span = slice(j * LANES, (j + 1) * LANES)
                nsend_ref[r, 3 * buckets + j : 3 * buckets + j + 1, :] = gains[:, span]
                nsend_ref[r, 3 * buckets + lanes + j : 3 * buckets + lanes + j + 1, :] = gain2_ref[:, span]

    event(12)(lambda: side_stage(0))

    @event(13)
    def _():
        far_stage(1)
        xf_out[0].start()
        out_out[1].start()

    @pl.when(u == steps - 1)
    def _():
        blk, cols = 16, 16 * 16
        same = lax.broadcasted_iota(I32, (blk, cols), 0) == (lax.broadcasted_iota(I32, (blk, cols), 1) & (blk - 1))
        picked = [
            jnp.sum(jnp.where(same, acc_ref[b * blk : (b + 1) * blk, :], 0.0), axis=0, keepdims=True)
            for b in range(3 * buckets)
        ]
        picked = jnp.concatenate(picked, axis=0)
        source = lax.broadcasted_iota(I32, (cols, LANES), 0) >> 4
        target = lax.broadcasted_iota(I32, (cols, LANES), 1)
        for r in range(4):
            choose = jnp.where((source == target + heads * r) & (target < heads), 1.0, 0.0).astype(F32)
            nsend_ref[r, : 3 * buckets, :] = jnp.dot(
                picked, choose, preferred_element_type=F32, precision=lax.Precision.HIGHEST
            )
        for copy in sn_out:
            copy.start()
        for copy in sn_out:
            copy.wait()
        nsend_ref[1] = nsend_ref[0] + nrecv_ref[0] + nrecv_ref[1] + nrecv_ref[2]
        sx_out.start()
        side_stage(1)
        sx_out.wait()
        nsend_ref[2] = nsend_ref[1] + sxrecv_ref[...]
        for r in range(1, ranks):
            sz_out[r].start()

        def finish(i):
            total = wide_f32(part_ref[i, rank, par])
            for r in range(1, ranks):
                za_out[i][r].wait_recv()
                total = total + wide_f32(zarecv_ref[i, r - 1])
            cols = slice(i * pw, (i + 1) * pw)
            gq_ref[:, cols] = total[:, :pw]
            gk_ref[:, cols] = total[:, pw : 2 * pw]
            gv_ref[:, cols] = total[:, 2 * pw : 3 * pw]
            go_ref[cols, :] = total[:, 3 * pw :].T

        finish(0)
        total = nsend_ref[2]
        for r in range(1, ranks):
            sz_out[r].wait_recv()
            total = total + szrecv_ref[r - 1]
        small_ref[...] = total
        ffn_stage(0)
        for r in range(1, ranks):
            zf_out[r].wait_recv()
        for m, ref in enumerate((fg_ref, fu_ref, fd_ref)):
            total = wide_f32(xfrecv_ref[0, m])
            for r in range(1, ranks):
                total = total + wide_f32(zfrecv_ref[r - 1, m])
            ref[...] = total.T
        finish(1)
        for copy in out_out:
            copy.wait()
        for copy in core_out + far_out[0] + far_out[1] + xf_out + zf_out[1:] + xa_out + za_out[0][1:] + za_out[1][1:] + sz_out[1:]:
            copy.wait_send()


def backward(wide, buckets, ga, x, gain, gain2, fsum, gm, e, ids, out, wo_all, ctx, linv, qkv, w_all, trows=64):
    slots, d = x.shape
    heads = 4
    pw = 2 * HEAD_DIM
    ranks, chunk = wide // 2, d // wide
    ff = fsum.shape[-1]
    width = heads * HEAD_DIM
    small = 3 * buckets + 2 * d // LANES
    vmem, anywhere = pl.BlockSpec(memory_space=pltpu.VMEM), pl.BlockSpec(memory_space=pl.ANY)
    shape = jax.ShapeDtypeStruct
    dma = pltpu.SemaphoreType.DMA

    def slot(u):
        k = jnp.minimum(u, 7)
        return 6 - 2 * (k >> 1) + (k & 1)

    return pl.pallas_call(
        functools.partial(backward_kernel, wide, heads, buckets, trows),
        grid=(8 + slots // trows,),
        in_specs=[vmem] * 5 + [anywhere] * 6 + [
            pl.BlockSpec((pw, d), lambda u: (slot(u), 0)),
            pl.BlockSpec((slots, pw), lambda u: (0, slot(u))),
            pl.BlockSpec((slots, pw), lambda u: (0, slot(u))),
            pl.BlockSpec((3, slots, pw), lambda u: (0, 0, slot(u))),
            pl.BlockSpec((3, d, pw), lambda u: (0, 0, slot(u))),
        ],
        out_specs=[vmem, anywhere] + [vmem] * 8,
        out_shape=[
            shape((slots, d), F32),
            shape((slots, d), BF),
            shape((small, LANES), F32),
            shape((chunk, width), F32),
            shape((chunk, width), F32),
            shape((chunk, width), F32),
            shape((width, chunk), F32),
            shape((ff, chunk), F32),
            shape((ff, chunk), F32),
            shape((ff, chunk), F32),
        ],
        scratch_shapes=[
            pltpu.VMEM((8, 2, slots, slots), BF),
            pltpu.VMEM((3, slots, slots), I32),
            pltpu.VMEM((d, slots), BF),
            pltpu.VMEM((d, slots), BF),
            pltpu.VMEM((slots, d), F32),
            pltpu.VMEM((3 * buckets * 16, 16 * 16), F32),
            pltpu.VMEM((8, ranks, 2, chunk, 4 * pw), BF),
            pltpu.VMEM((4, ranks, 2, chunk, 4 * pw), BF),
            pltpu.VMEM((2, ranks, 2, chunk, 4 * pw), BF),
            pltpu.VMEM((2, ranks, chunk, 4 * pw), BF),
            pltpu.VMEM((2, ranks - 1, chunk, 4 * pw), BF),
            pltpu.VMEM((ranks, 3, chunk, ff), BF),
            pltpu.VMEM((ranks - 1, 3, chunk, ff), BF),
            pltpu.VMEM((4, small, LANES), F32),
            pltpu.VMEM((3, small, LANES), F32),
            pltpu.VMEM((small, LANES), F32),
            pltpu.VMEM((ranks - 1, small, LANES), F32),
            dma((4,)), dma((2,)), dma((4, 2)), dma((2, 2, 2)), dma((2, 2)), dma((ranks, 2)), dma((ranks - 1, 2)),
            dma((2, 2)), dma((2, ranks - 1, 2)), dma((3, 2)), dma((2,)), dma((ranks - 1, 2)),
        ],
        compiler_params=pltpu.CompilerParams(
            vmem_limit_bytes=VMEM_LIMIT, collective_id=3, has_side_effects=True
        ),
        cost_estimate=pl.CostEstimate(flops=30 * slots * d * d, bytes_accessed=60 << 20, transcendentals=0),
        name="backward",
    )(ga, x, gain, gain2, fsum, gm, e, *ids, out, wo_all, ctx, linv, qkv, w_all)


def fixed_tables(tables):
    rows = jnp.concatenate([t.T for t in tables], axis=0).astype(F32)
    rows = jnp.round(rows * FIXED)
    return jnp.pad(rows, ((0, 16 - rows.shape[0]), (0, LANES - rows.shape[1])))


def shards(
    wide, narrow, hidden_in, grad_out, gain_attn, gain_ffn, w_query, w_key, w_value, w_output,
    table_rel, table_horiz, table_vert, wi_gate, wi_up, wo_ffn, counts, patch_mask,
    bucket_rel, bucket_horiz, bucket_vert,
):
    slots = bucket_rel.shape[1]
    rows, d = hidden_in.shape
    buckets, heads = table_rel.shape
    width = w_query.shape[1]
    ff = wi_gate.shape[1]
    assert rows == slots and narrow == 4 and heads * HEAD_DIM == width
    me = lax.axis_index("narrow").astype(I32)

    positions = jnp.arange(slots, dtype=I32)
    text = slots - patch_mask.shape[1]
    count = lax.dynamic_index_in_dim(counts, me, 0, False)
    patches = lax.dynamic_index_in_dim(patch_mask, me, 0, False)
    valid = jnp.concatenate([positions[:text] < count, patches == 1]).astype(F32)[:, None]
    ids = (bucket_rel, bucket_horiz, bucket_vert)

    gain_first = gain_attn.astype(F32)
    gain_second = gain_ffn.astype(F32)
    qkv, exps, context, linv, w_all, wo_all, middle, ffn_own, grad_far, wg_core, wu_core, wd_core = forward(
        hidden_in, gain_first[None], gain_second[None], valid, fixed_tables((table_rel, table_horiz, table_vert)),
        w_query, w_key, w_value, w_output, ids, grad_out, wi_gate.T, wi_up.T, wo_ffn,
    )
    out, ffn_sum, grad_middle, grad_attn, grad_gain_second = feed_forward(
        ffn_own, grad_out, grad_far, middle, gain_second[None],
        (wi_gate.T, wi_up.T, wo_ffn), (wg_core, wu_core, wd_core),
    )
    grad_input, out_in, small, gq, gk, gv, go, fg, fu, fd = backward(
        wide, buckets, grad_attn, hidden_in, gain_first[None], grad_gain_second,
        ffn_sum.reshape(3, wide // 2, 2, d // wide, ff), grad_middle, exps, ids, out,
        wo_all, context, linv, qkv, w_all,
    )
    block_out = (middle + (out[:slots].astype(F32) + out_in.astype(F32))).astype(BF)

    place = lax.axis_index("wide")
    per = d // (wide * narrow)
    gains = small[3 * buckets :].reshape(2, d)
    gains = lax.dynamic_slice_in_dim(gains, (place * narrow + me) * per, per, 1)
    tables = small[: 3 * buckets, :heads].reshape(3, buckets, heads)
    tables = lax.dynamic_slice_in_dim(tables, place * (buckets // wide), buckets // wide, 1)
    return (
        block_out, grad_input, gains[0], gains[1], gq, gk, gv, go,
        tables[0], tables[1], tables[2], fg.T, fu.T, fd,
    )


def solution(mesh):
    rows, both = P(("wide", "narrow"), None), P(("wide", "narrow"))
    cols, across = P(None, "narrow"), P("narrow", None)
    grid, turned = P("wide", "narrow"), P("narrow", "wide")
    pages = P("wide", None, None)
    return jax.shard_map(
        functools.partial(shards, mesh.shape["wide"], mesh.shape["narrow"]),
        mesh=mesh,
        in_specs=(
            rows, rows, P(), P(), cols, cols, cols, across, cols, cols, cols, cols, cols, across,
            P("wide"), P("wide", None), pages, pages, pages,
        ),
        out_specs=(
            rows, rows, both, both, grid, grid, grid, turned, grid, grid, grid, grid, grid, turned,
        ),
        check_vma=False,
    )
```

profile of v0, /device:TPU:0, one launch (start us, length us, event | category | flops | bytes accessed | tf_op | source)
XLA Modules:
  0.0 248.6 jit_solution(11183249845759888837)
XLA Ops:
  0.6 1.2 dynamic_slice.14
  1.9 0.6 slice_compare_fusion
  2.6 0.7 compare_bitcast_fusion
  3.3 0.9 copy.36.valid_ref
  4.1 1.3 broadcast_in_dim.17
  5.4 1.3 broadcast_in_dim.18
  6.7 0.7 multiply_round-nearest-even_fusion
  7.4 0.6 pad.4.tab_ref
  8.0 58.5 %forward.1 = (bf16[3,512,1024]{2,1,0:T(8,128)(2,1)}, bf16[8,2,512,512]{3,2,1,0:T(8,128)(2,1)}, bf16[512,1024]{1,0:T(8,128)(2,1)}, f32[512,1024]{1,0:T(8,128)}, b...) custom-call(bf16[512,1024]{1,0:T(8,128)(2,1)} %x_ref.3, ...), custom_call_target="tpu_custom_call" | custom-call | flops 10737418240 | bytes 41943040 | tf_op jit(solution)/shard_map/forward/pallas_call | solution.py:251
  66.5 55.5 %feed_forward.1 = (bf16[1024,1024]{1,0:T(8,128)(2,1)}, bf16[3,1024,704]{2,1,0:T(8,128)(2,1)}, f32[512,1024]{1,0:T(8,128)}, bf16[512,1024]{1,0:T(8,128)(2,1)}, f32[1,1024]{1,0:T(1,128)}) custom-call(bf16[512,1024]{1,0:T(8,128)(2,1)} %get-tuple-element.42.x_ref, bf16[512,1024]{1,0:T(8,128)(2,1)} %go_ref.3, bf16[512,1024]{1,0:T(8,128)(2,1)} %get-tuple-element.43.gofar_ref, ...), custom_call_target="tpu_custom_call" | custom-call | flops 13287555072 | bytes 41943040 | tf_op jit(solution)/shard_map/feed_forward/pallas_call | solution.py:418
  122.0 115.4 %backward.1 = (f32[512,1024]{1,0:T(8,128)}, bf16[512,1024]{1,0:T(8,128)(2,1)}, f32[112,128]{1,0:T(8,128)}, f32[128,256]{1,0:T(8,128)}, f32[128,256]{1,0:T(8,128)...) custom-call(bf16[512,1024]{1,0:T(8,128)(2,1)} %get-tuple-element.48., ...), custom_call_target="tpu_custom_call" | custom-call | flops 16106127360 | bytes 62914560 | tf_op jit(solution)/shard_map/backward/pallas_call | solution.py:749
  237.4 0.0 copy-start.8
  237.4 0.0 copy-start
  237.4 3.8 %add_convert_fusion = bf16[512,1024]{1,0:T(8,128)(2,1)} fusion(f32[512,1024]{1,0:T(8,128)} %get-tuple-element.41.middle_ref, bf16[512,1024]{1,0:T(8,128)(2,1)} %get-tuple-element.58, bf16[1024,1024]{1,0:T(8,128)(2,1)} %get-tuple-element.47.out_ref), kind=kLoop, calls=%fused_computation | loop fusion | flops 2621440 | bytes 5242880 | tf_op jit(solution)/shard_map/convert_element_type | solution.py:842
  241.2 0.0 copy-done.8
  241.2 0.6 dynamic-slice_bitcast_fusion
  241.8 0.1 constant_dynamic-slice_fusion
  241.9 0.5 slice_bitcast_fusion
  242.4 0.0 copy-done
  242.4 0.0 copy-start.7
  242.4 0.0 copy-start.6
  242.4 0.0 copy-start.5
  242.4 0.0 copy-start.4
  242.4 0.0 copy-start.3
  242.5 0.0 copy-start.2
  242.5 1.3 copy.45
  243.8 0.0 copy-done.7
  243.8 0.0 copy-start.1
  243.8 0.7 copy.46
  244.4 0.0 copy-done.6
  244.4 0.7 copy.47
  245.1 0.0 copy-done.5
  245.1 0.7 copy.48
  245.8 0.0 copy-done.4
  245.8 0.7 copy.49
  246.4 0.0 copy-done.3
  246.4 0.7 copy.50
  247.2 0.0 copy-done.2
  247.2 0.7 copy.51
  247.9 0.0 copy-done.1
  247.9 0.7 copy.52
  (6 shorter events, 0.0 us)
Async XLA Ops:
  237.4 3.8 %copy-start.8 = (f32[112,128]{1,0:T(8,128)S(1)}, f32[112,128]{1,0:T(8,128)}, u32[]{:S(2)}) copy-start(f32[112,128]{1,0:T(8,128)} %get-tuple-element.60) | copy-start | bytes 172036
  237.4 5.0 %copy-start = (f32[512,1024]{1,0:T(8,128)S(1)}, f32[512,1024]{1,0:T(8,128)}, u32[]{:S(2)}) copy-start(f32[512,1024]{1,0:T(8,128)} %get-tuple-element.88) | copy-start | bytes 6291460
  242.4 1.4 copy-start.7
  242.4 2.0 copy-start.6
  242.4 2.7 %copy-start.5 = (f32[128,256]{1,0:T(8,128)S(1)}, f32[128,256]{1,0:T(8,128)}, u32[]{:S(2)}) copy-start(f32[128,256]{1,0:T(8,128)} %get-tuple-element.93) | copy-start | bytes 393220
  242.4 3.3 %copy-start.4 = (f32[256,128]{1,0:T(8,128)S(1)}, f32[256,128]{1,0:T(8,128)}, u32[]{:S(2)}) copy-start(f32[256,128]{1,0:T(8,128)} %get-tuple-element.94) | copy-start | bytes 393220
  242.4 4.0 %copy-start.3 = (f32[704,128]{1,0:T(8,128)S(1)}, f32[704,128]{1,0:T(8,128)}, u32[]{:S(2)}) copy-start(f32[704,128]{1,0:T(8,128)} %get-tuple-element.65) | copy-start | bytes 1081348
  242.5 4.7 %copy-start.2 = (f32[704,128]{1,0:T(8,128)S(1)}, f32[704,128]{1,0:T(8,128)}, u32[]{:S(2)}) copy-start(f32[704,128]{1,0:T(8,128)} %get-tuple-element.66) | copy-start | bytes 1081348
  243.8 4.1 %copy-start.1 = (f32[704,128]{1,0:T(8,128)S(1)}, f32[704,128]{1,0:T(8,128)}, u32[]{:S(2)}) copy-start(f32[704,128]{1,0:T(8,128)} %get-tuple-element.100) | copy-start | bytes 1081348
where the time goes:
time: 249 us
  Pallas kernels  229 us (92%)
  local copies, waits for them, and re-layouts  10.1 us (4%)
  other arithmetic  8.43 us (3%)
    pallas_call x1, Pallas kernels, backward(): pl.pallas_call(functools.partial(backward_kernel, wide, heads, buckets, t...  115 us
    pallas_call x1, Pallas kernels, forward(): pl.pallas_call(functools.partial(forward_kernel, heads, chunk), in_specs=...  58.5 us
    pallas_call x1, Pallas kernels, feed_forward(): pl.pallas_call(functools.partial(ffn_kernel, block), in_specs=[anywhere]...  55.5 us
    unnamed x26, local copies, waits for them, and re-layouts  6.18 us

commit v1 on v0

v1 whole, which is shorter than its diff:
```python
import functools
import math

import jax
import jax.numpy as jnp
from jax import lax
from jax.experimental import pallas as pl
from jax.experimental.pallas import tpu as pltpu
from jax.sharding import PartitionSpec as P

F32 = jnp.float32
BF = jnp.bfloat16
I32 = jnp.int32
HEAD_DIM = 64
LANES = 128
EPS = 1e-06
NT = (((1,), (1,)), ((), ()))

FIXED = 2048.0
OFFSET = 8192
MASKED = -3.0e12
VMEM_LIMIT = 60 << 20
MESH = pl.DeviceIdType.MESH


def lookup(table_row, ids):
    return jnp.take_along_axis(table_row, ids, axis=1, mode="promise_in_bounds")


def neighbours():
    w, n = lax.axis_index("wide"), lax.axis_index("narrow")
    return w, n, (w, n ^ 1), (w, n ^ 2), (w, n ^ 3), (w ^ 1, n)


def greet(devices):
    barrier = pltpu.get_barrier_semaphore()
    for device in devices:
        pl.semaphore_signal(barrier, inc=1, device_id=device, device_id_type=MESH)
    pl.semaphore_wait(barrier, len(devices))


def remote(src, dst, sems, device):
    return pltpu.make_async_remote_copy(
        src_ref=src, dst_ref=dst, send_sem=sems.at[0], recv_sem=sems.at[1], device_id=device, device_id_type=MESH
    )


def forward_kernel(
    heads, buckets, chunk,
    counts_ref, patch_ref, x_ref, gain1_ref, gain2_ref, tr_ref, th_ref, tv_ref,
    wq_ref, wk_ref, wv_ref, wo_ref, ir_ref, ih_ref, iv_ref, go_ref, wg_ref, wu_ref, wd_ref,
    qkv_ref, e_ref, ctx_ref, linv_ref, wall_ref, woall_ref, middle_ref, ffn_ref, gofar_ref, wgc_ref, wuc_ref, wdc_ref,
    normed_ref, mask_ref, ids_ref, tab_ref, tabs_ref, words_ref, ebuf_ref,
    own_sem, id_sem, e_sem, core_sem, far_sem, deep_sem, wide_sem, fwd_sem, tab_sem, big_sem,
):
    pw = 2 * HEAD_DIM
    slots, d = x_ref.shape
    piece = d // 2
    w, n, core, far, diag, side = neighbours()
    deep = (w ^ 2, n)
    half, share = w & 1, (w >> 1) & 1
    other = 1 - half

    def source(m, pair, part=None):
        cols = pl.ds(pl.multiple_of(pair * pw, pw), pw)
        span = slice(None) if part is None else pl.ds(pl.multiple_of(part * piece, piece), piece)
        return wo_ref.at[cols, span] if m == 3 else (wq_ref, wk_ref, wv_ref)[m].at[span, cols]

    def place(m, slot, part=None):
        cols = pl.ds(pl.multiple_of(slot * pw, pw), pw)
        span = slice(None) if part is None else pl.ds(pl.multiple_of(part * piece, piece), piece)
        return woall_ref.at[cols, span] if m == 3 else wall_ref.at[m, span, cols]

    ids_in = [pltpu.make_async_copy(r.at[n], ids_ref.at[t], id_sem.at[t]) for t, r in enumerate((ir_ref, ih_ref, iv_ref))]
    own_in = [[pltpu.make_async_copy(source(m, p), place(m, p), own_sem.at[p, m]) for m in range(4)] for p in range(2)]
    for copy in own_in[0][:3] + ids_in + own_in[0][3:] + own_in[1]:
        copy.start()

    tab_ref[...] = jnp.zeros_like(tab_ref)
    for t, r in enumerate((tr_ref, th_ref, tv_ref)):
        tab_ref[t * heads : (t + 1) * heads, :buckets] = jnp.floor(r[...].astype(F32) * FIXED + 0.5)

    greet((core, far, diag, side, deep))
    far_out = [remote(source(m, half, share), place(m, 4 + half, share), far_sem.at[m], far) for m in range(4)]
    deep_out = [remote(place(m, 4 + half, share), place(m, 4 + half, share), deep_sem.at[m], deep) for m in range(4)]
    core_out = [[remote(source(m, p), place(m, 2 + p), core_sem.at[p, m], core) for m in range(4)] for p in range(2)]
    tabs_out = [remote(tab_ref, tabs_ref.at[r - 1], tab_sem.at[r - 1], dev) for r, dev in ((1, core), (2, far), (3, diag))]
    wide_out = [
        [remote(place(m, 4 + half, k), place(m, 4 + half, k), wide_sem.at[m, i], side) for i, k in enumerate((share, 1 - share))]
        for m in range(4)
    ]
    fwd_out = [
        [remote(place(m, 4 + half, k), place(m, 6 + half, k), fwd_sem.at[m, i], core) for i, k in enumerate((share, 1 - share))]
        for m in range(4)
    ]
    last_out = [remote(place(m, 4 + other), place(m, 6 + other), fwd_sem.at[m, 2], core) for m in range(4)]
    go_out = remote(go_ref, gofar_ref, big_sem.at[0], far)
    ffn_out = [
        remote(wg_ref, wgc_ref, big_sem.at[1], core),
        remote(wu_ref, wuc_ref, big_sem.at[2], core),
        remote(wd_ref, wdc_ref, big_sem.at[3], core),
    ]
    for copy in tabs_out + far_out + [go_out] + core_out[0] + core_out[1]:
        copy.start()

    x = x_ref[...].astype(F32)
    inv = lax.rsqrt(jnp.mean(x * x, axis=-1, keepdims=True) + EPS)
    normed_ref[...] = (x * inv * gain1_ref[...].astype(F32)[None]).astype(BF)
    text = slots - patch_ref.shape[1]
    shown = jnp.concatenate(
        [
            jnp.where(lax.broadcasted_iota(I32, (1, text), 1) < counts_ref[n], 1, 0),
            patch_ref[pl.ds(n, 1), :],
        ],
        axis=1,
    )
    column = jnp.broadcast_to(jnp.where(shown == 1, 0.0, MASKED), (pw, slots)).T
    lane_all = lax.broadcasted_iota(I32, (slots, pw), 1)
    mask_ref[...] = jnp.where(lane_all == 0, column, 0.0).astype(BF)
    ones = jnp.ones((slots, pw), BF)
    lane = lax.broadcasted_iota(I32, (chunk, pw), 1)
    low = lane < HEAD_DIM
    first = jnp.where(lane == 0, 1.0, 0.0).astype(BF)
    to_log2 = math.log2(math.e) / FIXED

    def pack_words(r, table):
        fixed = table.astype(I32)
        for p in range(2):
            for t in range(3):
                row = t * heads + 2 * p
                words_ref[2 * r + p, t : t + 1, :] = fixed[row + 1 : row + 2] * 65536 + fixed[row : row + 1] + OFFSET

    pack_words(0, tab_ref[...])
    for copy in ids_in:
        copy.wait()

    def e_out(parity, slot):
        return pltpu.make_async_copy(ebuf_ref.at[parity], e_ref.at[slot], e_sem.at[parity])

    def slot_of(t):
        late = 4 + 2 * (t & 1) + jnp.where(t >= 6, other, half)
        return jnp.where(t < 4, t, late)

    plan = [[] for _ in range(16)]

    def far_arrived(m):
        far_out[m].wait_recv()
        deep_out[m].start()
        wide_out[m][0].start()
        fwd_out[m][0].start()

    def deep_arrived(m):
        deep_out[m].wait_recv()
        wide_out[m][1].start()
        fwd_out[m][1].start()

    def wide_arrived(m):
        for copy in wide_out[m]:
            copy.wait_recv()
        last_out[m].start()

    def tables_arrived():
        for r, copy in enumerate(tabs_out):
            copy.wait()
            pack_words(r + 1, tabs_ref[r])

    for p in range(2):
        plan[2 * p].extend(own_in[p][m].wait for m in range(3))
        plan[4 + 2 * p].extend(core_out[p][m].wait_recv for m in range(3))
    plan[3].append(tables_arrived)
    for m in range(4):
        plan[2 + m].append(functools.partial(far_arrived, m))
        plan[4 + m].append(functools.partial(deep_arrived, m))
    plan[7].extend(copy.start for copy in ffn_out)
    plan[10].extend(copy.wait_recv for m in range(3) for copy in fwd_out[m])
    plan[12].extend(functools.partial(wide_arrived, m) for m in range(3))
    plan[14].extend(last_out[m].wait_recv for m in range(3))
    plan[14].append(functools.partial(wide_arrived, 3))

    def events(t, c):
        for k in range(8):
            if plan[2 * k + c]:

                @pl.when(t == k)
                def _():
                    for action in plan[2 * k + c]:
                        action()

    def step(t, carry):
        slot = slot_of(t)
        events(t, 0)
        parity = t & 1

        @pl.when(t >= 2)
        def _():
            e_out(parity, slot).wait()

        cols = pl.ds(pl.multiple_of(slot * pw, pw), pw)
        weights = jnp.concatenate([wall_ref[m, :, cols] for m in range(3)], axis=1)
        joined = jnp.dot(normed_ref[...], weights, preferred_element_type=F32).astype(BF)
        for m in range(3):
            qkv_ref[m, :, cols] = joined[:, m * pw : (m + 1) * pw]
        kx = jnp.concatenate([joined[:, pw : 2 * pw], mask_ref[...]], axis=1)
        vx = jnp.concatenate([joined[:, 2 * pw :], ones], axis=1)
        words = words_ref[slot]
        for c in range(slots // chunk):
            if c == slots // chunk // 2:
                events(t, 1)
            rows = slice(c * chunk, (c + 1) * chunk)
            q2 = joined[rows, :pw] * jnp.bfloat16(FIXED)
            zero = jnp.zeros_like(q2)
            scores = []
            for sub in range(2):
                q = jnp.where(low, q2, zero) if sub == 0 else jnp.where(low, zero, q2)
                q = jnp.concatenate([q, first], axis=1)
                scores.append(lax.dot_general(q, kx, NT, preferred_element_type=F32))
            tabs = [jnp.broadcast_to(words[k : k + 1, :], (chunk, LANES)) for k in range(3)]
            parts = ([], [])
            for j in range(slots // LANES):
                sl = slice(j * LANES, (j + 1) * LANES)
                bias = (
                    lookup(tabs[0], ids_ref[0, rows, sl])
                    + lookup(tabs[1], ids_ref[1, rows, sl])
                    + lookup(tabs[2], ids_ref[2, rows, sl])
                )
                parts[0].append(scores[0][:, sl] + (bias & 0xFFFF).astype(F32))
                parts[1].append(scores[1][:, sl] + (bias >> 16).astype(F32))
            outs = []
            for sub in range(2):
                s = jnp.concatenate(parts[sub], axis=1)
                peak = jnp.max(s, axis=1, keepdims=True)
                e = jnp.exp2((s - peak) * to_log2).astype(BF)
                ebuf_ref[parity, sub, rows, :] = e
                outs.append(jnp.dot(e, vx, preferred_element_type=F32))
            linv = 1.0 / jnp.where(low, outs[0][:, pw:], outs[1][:, pw:])
            linv_ref[rows, cols] = linv
            ctx_ref[rows, cols] = (jnp.where(low, outs[0][:, :pw], outs[1][:, :pw]) * linv).astype(BF)
        e_out(parity, slot).start()
        return carry

    lax.fori_loop(0, 8, step, 0)
    for p in range(2):
        own_in[p][3].wait()
        core_out[p][3].wait_recv()
    for copy in fwd_out[3] + last_out[3:]:
        copy.wait_recv()
    middle = x_ref[...].astype(F32) + jnp.dot(ctx_ref[...], woall_ref[...], preferred_element_type=F32)
    middle_ref[...] = middle
    inv = lax.rsqrt(jnp.mean(middle * middle, axis=-1, keepdims=True) + EPS)
    ffn_ref[...] = (middle * inv * gain2_ref[...].astype(F32)[None]).astype(BF)
    for p in range(2):
        e_out(p, p).wait()
        for m in range(4):
            core_out[p][m].wait_send()
    for m in range(4):
        for copy in [far_out[m], deep_out[m], last_out[m]] + wide_out[m] + fwd_out[m]:
            copy.wait_send()
    for copy in ffn_out:
        copy.wait()
    go_out.wait()


def forward(counts, patches, x, gain1, gain2, tables, wq, wk, wv, wo, ids, grad_out, wg, wu, wd, chunk=256):
    slots, d = x.shape
    heads = wq.shape[1] // HEAD_DIM
    buckets = tables[0].shape[1]
    ff = wd.shape[0]
    assert heads == 4
    vmem, anywhere = pl.BlockSpec(memory_space=pltpu.VMEM), pl.BlockSpec(memory_space=pl.ANY)
    shape = jax.ShapeDtypeStruct
    dma = pltpu.SemaphoreType.DMA
    return pl.pallas_call(
        functools.partial(forward_kernel, heads, buckets, chunk),
        in_specs=[pl.BlockSpec(memory_space=pltpu.SMEM)] + [vmem] * 7 + [anywhere] * 11,
        out_specs=[vmem, anywhere] + [vmem] * 6 + [anywhere] * 4,
        out_shape=[
            shape((3, slots, d), BF),
            shape((8, 2, slots, slots), BF),
            shape((slots, d), BF),
            shape((slots, d), F32),
            shape((3, d, d), BF),
            shape((d, d), BF),
            shape((slots, d), F32),
            shape((slots, d), BF),
            shape((slots, d), BF),
            shape((ff, d), BF),
            shape((ff, d), BF),
            shape((ff, d), BF),
        ],
        scratch_shapes=[
            pltpu.VMEM((slots, d), BF),
            pltpu.VMEM((slots, 2 * HEAD_DIM), BF),
            pltpu.VMEM((3, slots, slots), I32),
            pltpu.VMEM((16, LANES), F32),
            pltpu.VMEM((3, 16, LANES), F32),
            pltpu.VMEM((8, 8, LANES), I32),
            pltpu.VMEM((2, 2, slots, slots), BF),
            dma((2, 4)), dma((3,)), dma((2,)), dma((2, 4, 2)), dma((4, 2)), dma((4, 2)), dma((4, 2, 2)), dma((4, 3, 2)),
            dma((3, 2)), dma((4, 2)),
        ],
        compiler_params=pltpu.CompilerParams(
            vmem_limit_bytes=VMEM_LIMIT, collective_id=1, has_side_effects=True
        ),
        cost_estimate=pl.CostEstimate(flops=20 * slots * d * d, bytes_accessed=40 << 20, transcendentals=16 * slots * slots),
        name="forward",
    )(counts, patches, x, gain1, gain2, *tables, wq, wk, wv, wo, *ids, grad_out, wg, wu, wd)


def gelu_parts(v):
    c, k = math.sqrt(2.0 / math.pi), 0.044715
    square = v * v
    t = jnp.tanh(c * v * (1.0 + k * square))
    up = 0.5 * (1.0 + t)
    slope = up + 0.5 * v * (1.0 - t * t) * (c * (1.0 + 3.0 * k * square))
    return v * up, slope


def split_quarter(ff):
    return ff // LANES * LANES, ff % LANES


def packed_width(ff):
    full, rest = split_quarter(ff)
    return 3 * full + -(-3 * rest // LANES) * LANES


def ffn_kernel(
    block, ff,
    x_ref, go_ref, gofar_ref, middle_ref, gain_ref, w0_ref, w1_ref, w2_ref, c0_ref, c1_ref, c2_ref,
    out_ref, sum_ref, gm_ref, ga_ref, gain_out_ref,
    xall_ref, gall_ref, wgu_ref, wd_ref, xt_ref, gt_ref, act_ref, send_ref, recv_ref, own_ref, backfar_ref, backin_ref,
    in_sem, w_sem, x_sem, back_sem, dw_sem,
):
    slots, d = middle_ref.shape
    halves = slots // block
    full, rest = split_quarter(ff)
    both = 2 * ff
    _, _, core, far, _, _ = neighbours()

    ins = [
        pltpu.make_async_copy(x_ref, xall_ref.at[pl.ds(0, slots), :], in_sem.at[0]),
        pltpu.make_async_copy(go_ref, gall_ref.at[pl.ds(0, slots), :], in_sem.at[1]),
        pltpu.make_async_copy(gofar_ref, gall_ref.at[pl.ds(slots, slots), :], in_sem.at[2]),
    ]
    weights = []
    for m, pair in enumerate(((w0_ref, c0_ref), (w1_ref, c1_ref), (w2_ref, c2_ref))):
        target, base = (wd_ref, 0) if m == 2 else (wgu_ref, m * both)
        for q, r in enumerate(pair):
            for k, (start, size, at) in enumerate(((0, full, q * full), (full, rest, 2 * full + q * rest))):
                if size:
                    weights.append(
                        pltpu.make_async_copy(
                            r.at[pl.ds(start, size), :], target.at[pl.ds(base + at, size), :], w_sem.at[m, q, k]
                        )
                    )
    for copy in ins[:2] + weights + ins[2:]:
        copy.start()
    greet((core, far))
    x_out = [
        remote(x_ref.at[pl.ds(i * block, block), :], xall_ref.at[pl.ds(slots + i * block, block), :], x_sem.at[i], far)
        for i in range(halves)
    ]
    for copy in x_out:
        copy.start()
    back_out = [
        remote(backfar_ref.at[pl.ds(i * block, block), :], backin_ref.at[pl.ds(i * block, block), :], back_sem.at[i], far)
        for i in range(halves)
    ]
    for copy in ins + weights:
        copy.wait()

    def step(b, carry):
        for i in range(halves):

            @pl.when(b == halves + i)
            def _():
                x_out[i].wait_recv()

        rows = pl.ds(pl.multiple_of(b * block, block), block)
        x, g = xall_ref[rows, :], gall_ref[rows, :]
        xt_ref[:, rows] = x.T
        gt_ref[:, rows] = g.T
        grown = lax.dot_general(x, wgu_ref[...], NT, preferred_element_type=F32)
        grad_hidden = lax.dot_general(g, wd_ref[...], NT, preferred_element_type=F32)
        gate, upper = grown[:, :both], grown[:, both:]
        gelu, slope = gelu_parts(gate)
        dg = (grad_hidden * upper * slope).astype(BF)
        du = (grad_hidden * gelu).astype(BF)
        hidden = (gelu * upper).astype(BF)
        act_ref[0, rows, :] = dg
        act_ref[1, rows, :] = du
        act_ref[2, rows, :] = hidden
        back = jnp.dot(jnp.concatenate([dg, du], axis=1), wgu_ref[...], preferred_element_type=F32)

        @pl.when(b < halves)
        def _():
            own_ref[rows, :] = back

        for i in range(halves):

            @pl.when(b == halves + i)
            def _():
                backfar_ref[i * block : (i + 1) * block, :] = back.astype(BF)
                back_out[i].start()

        out_ref[rows, :] = jnp.dot(hidden, wd_ref[...], preferred_element_type=F32).astype(BF)
        return carry

    lax.fori_loop(0, 2 * halves, step, 0)

    tile = d // 2
    used = 3 * (full + rest)
    dw_out = [
        remote(send_ref.at[pl.ds(c * tile, tile), :], recv_ref.at[pl.ds(c * tile, tile), :], dw_sem.at[c], core)
        for c in range(2)
    ]
    for c in range(2):
        rows = slice(c * tile, (c + 1) * tile)
        for m in range(3):
            left = gt_ref if m == 2 else xt_ref
            dw = jnp.dot(left[rows, :], act_ref[m], preferred_element_type=F32).astype(BF)
            for q, target in enumerate((sum_ref, send_ref)):
                target[rows, m * full : (m + 1) * full] = dw[:, q * full : (q + 1) * full]
                if rest:
                    at = 2 * full + q * rest
                    target[rows, 3 * full + m * rest : 3 * full + (m + 1) * rest] = dw[:, at : at + rest]
        for target in (sum_ref, send_ref):
            if used < target.shape[1]:
                target[rows, used:] = jnp.zeros((tile, target.shape[1] - used), BF)
        dw_out[c].start()
    for c in range(2):
        rows = slice(c * tile, (c + 1) * tile)
        dw_out[c].wait_recv()
        sum_ref[rows, :] = (sum_ref[rows, :].astype(F32) + recv_ref[rows, :].astype(F32)).astype(BF)

    for copy in back_out:
        copy.wait_recv()
    middle = middle_ref[...]
    inv = lax.rsqrt(jnp.mean(middle * middle, axis=-1, keepdims=True) + EPS)
    upstream = own_ref[...] + backin_ref[...].astype(F32)
    lifted = upstream * gain_ref[...].astype(F32)[None]
    inner = jnp.mean(lifted * middle, axis=-1, keepdims=True)
    gain_out_ref[...] = jnp.sum(upstream * middle * inv, axis=0, keepdims=True)
    gm = gall_ref[0:slots, :].astype(F32) + inv * lifted - middle * (inv * inv * inv * inner)
    gm_ref[...] = gm
    ga_ref[...] = gm.astype(BF)
    for copy in x_out + back_out + dw_out:
        copy.wait_send()


def feed_forward(x, go, gofar, middle, gain, own, other, block=256):
    slots, d = x.shape
    ff = own[0].shape[0]
    vmem, anywhere = pl.BlockSpec(memory_space=pltpu.VMEM), pl.BlockSpec(memory_space=pl.ANY)
    shape = jax.ShapeDtypeStruct
    dma = pltpu.SemaphoreType.DMA
    halves = slots // block
    packed = packed_width(ff)
    return pl.pallas_call(
        functools.partial(ffn_kernel, block, ff),
        in_specs=[anywhere] * 3 + [vmem] * 2 + [anywhere] * 6,
        out_specs=[vmem] * 5,
        out_shape=[
            shape((2 * slots, d), BF),
            shape((d, packed), BF),
            shape((slots, d), F32),
            shape((slots, d), BF),
            shape((1, d), F32),
        ],
        scratch_shapes=[
            pltpu.VMEM((2 * slots, d), BF),
            pltpu.VMEM((2 * slots, d), BF),
            pltpu.VMEM((4 * ff, d), BF),
            pltpu.VMEM((2 * ff, d), BF),
            pltpu.VMEM((d, 2 * slots), BF),
            pltpu.VMEM((d, 2 * slots), BF),
            pltpu.VMEM((3, 2 * slots, 2 * ff), BF),
            pltpu.VMEM((d, packed), BF),
            pltpu.VMEM((d, packed), BF),
            pltpu.VMEM((slots, d), F32),
            pltpu.VMEM((slots, d), BF),
            pltpu.VMEM((slots, d), BF),
            dma((3,)), dma((3, 2, 2)), dma((halves, 2)), dma((halves, 2)), dma((2, 2)),
        ],
        compiler_params=pltpu.CompilerParams(
            vmem_limit_bytes=VMEM_LIMIT, collective_id=2, has_side_effects=True
        ),
        cost_estimate=pl.CostEstimate(flops=36 * slots * d * ff, bytes_accessed=40 << 20, transcendentals=4 * slots * ff),
        name="feed_forward",
    )(x, go, gofar, middle, gain, *own, *other)


def backward_slot(k):
    return jnp.where(k < 4, 6 - 2 * (k & 1) + (k >> 1), 6 - 2 * (k >> 1) + (k & 1))


def backward_kernel(
    wide, heads, buckets, trows, ff,
    ga_ref, x_ref, gain_ref, gain2_ref, fsum_ref, gm_ref, e_ref, ir_ref, ih_ref, iv_ref, out_ref,
    wo_ref, ctx_ref, linv_ref, qkv_ref, wall_ref,
    gi_ref, outin_ref, small_ref, gq_ref, gk_ref, gv_ref, go_ref, fg_ref, fu_ref, fd_ref,
    ds_ref, ids_ref, nt_ref, gat_ref, dx_ref, acc_ref, part_ref, crecv_ref, frecv_ref, xarecv_ref, zarecv_ref,
    xfrecv_ref, zfrecv_ref, nsend_ref, nrecv_ref, sxrecv_ref, szrecv_ref,
    in_sem, e_sem, core_sem, far_sem, out_sem, xf_sem, zf_sem, xa_sem, za_sem, sn_sem, sx_sem, sz_sem,
):
    pw = 2 * HEAD_DIM
    slots, d = ga_ref.shape
    half_rows = slots // 2
    ranks = wide // 2
    chunk = d // wide
    steps = 8 + slots // trows
    u = pl.program_id(0)
    w, n, core, far, diag, side = neighbours()
    par, rank = w & 1, w >> 1
    opp = 1 - par
    peer = lambda r: (2 * (rank ^ r) + par, n)
    slot_of = backward_slot
    slot = slot_of(jnp.minimum(u, 7))

    ins = [pltpu.make_async_copy(r.at[n], ids_ref.at[t], in_sem.at[t]) for t, r in enumerate((ir_ref, ih_ref, iv_ref))]
    gm_in = pltpu.make_async_copy(gm_ref, gi_ref, in_sem.at[3])
    core_out = [remote(part_ref.at[s], crecv_ref.at[i], core_sem.at[i], core) for i, s in enumerate((6, 7, 2, 3))]
    order = list(range(ranks - 1, 0, -2)) + list(range(ranks - 2, -1, -2))
    far_out = [
        [
            [
                remote(part_ref.at[4 + i, rank ^ r, p], frecv_ref.at[i, rank ^ r, p], far_sem.at[i, k, r], far)
                for r in range(ranks)
            ]
            for k, p in enumerate((opp, par))
        ]
        for i in range(2)
    ]
    out_out = [
        remote(
            out_ref.at[pl.ds(slots + i * half_rows, half_rows), :],
            outin_ref.at[pl.ds(i * half_rows, half_rows), :], out_sem.at[i], far,
        )
        for i in range(2)
    ]
    xf_out = [None] + [remote(fsum_ref.at[rank ^ r, opp], xfrecv_ref.at[r], xf_sem.at[r], side) for r in range(1, ranks)]
    some = chunk // 2
    xf_last = [
        remote(
            fsum_ref.at[rank, opp, pl.ds(k * some, some), :], xfrecv_ref.at[0, pl.ds(k * some, some), :],
            xf_sem.at[k * ranks], side,
        )
        for k in range(2)
    ]
    low_bit = lambda r: r & -r
    zf_out = [None] + [
        remote(xfrecv_ref.at[r], zfrecv_ref.at[r - 1], zf_sem.at[r - 1], peer(low_bit(r))) for r in range(1, ranks)
    ]
    feeds = lambda r: [r | (1 << b) for b in range(ranks.bit_length() - 1) if (1 << b) < (low_bit(r) if r else ranks)]
    xa_out = [
        [remote(part_ref.at[i, rank ^ r, opp], xarecv_ref.at[i, r], xa_sem.at[i, r], side) for r in range(ranks)]
        for i in range(2)
    ]
    za_out = [
        [None]
        + [
            remote(part_ref.at[i, rank ^ r, par], zarecv_ref.at[i, r - 1], za_sem.at[i, r - 1], peer(low_bit(r)))
            for r in range(1, ranks)
        ]
        for i in range(2)
    ]
    sn_out = [
        remote(nsend_ref.at[r], nrecv_ref.at[r - 1], sn_sem.at[r - 1], dev) for r, dev in ((1, core), (2, far), (3, diag))
    ]
    sx_out = remote(nsend_ref.at[1], sxrecv_ref, sx_sem, side)
    sz_out = [None] + [remote(nsend_ref.at[2], szrecv_ref.at[r - 1], sz_sem.at[r - 1], peer(r)) for r in range(1, ranks)]

    def e_in(k):
        s = slot_of(k)
        return pltpu.make_async_copy(e_ref.at[s], ds_ref.at[s], e_sem.at[k & 1])

    def wide_f32(ref_value):
        return ref_value.astype(F32)

    @pl.when(u == 0)
    def _():
        e_in(0).start()
        for copy in ins + [gm_in]:
            copy.start()
        greet([core, far, diag, side] + [peer(r) for r in range(1, ranks)])
        for r in range(ranks - 1, 0, -1):
            xf_out[r].start()
        out_out[0].start()
        x = x_ref[...].astype(F32)
        inv = lax.rsqrt(jnp.mean(x * x, axis=-1, keepdims=True) + EPS)
        nt_ref[...] = (x * inv * gain_ref[...].astype(F32)[None]).astype(BF).T
        gat_ref[...] = ga_ref[...].T
        dx_ref[...] = jnp.zeros_like(dx_ref)
        acc_ref[...] = jnp.zeros_like(acc_ref)

    @pl.when(u < 8)
    def _():
        e_in(u).wait()

        @pl.when(u < 7)
        def _():
            e_in(u + 1).start()

        lane = lax.broadcasted_iota(I32, (slots, pw), 1)
        low = lane < HEAD_DIM
        do2 = (lax.dot_general(ga_ref[...], wo_ref[...], NT, preferred_element_type=F32) * linv_ref[...]).astype(BF)
        prod = do2.astype(F32) * ctx_ref[...].astype(F32)
        q2, k2, v2 = qkv_ref[0], qkv_ref[1], qkv_ref[2]
        vx = jnp.concatenate([v2, jnp.where(lane < 2, 1.0, 0.0).astype(BF)], axis=1)
        do_t, q_t = do2.T, q2.T
        zero = jnp.zeros_like(do2)
        dq, dk, dv = [], [], []
        for sub in range(2):
            mine = low if sub == 0 else jnp.logical_not(low)
            row = -jnp.sum(jnp.where(mine, prod, 0.0), axis=1, keepdims=True)
            head_part = row.astype(BF).astype(F32)
            extra = jnp.where(lane == 0, head_part, jnp.where(lane == 1, row - head_part, 0.0)).astype(BF)
            dox = jnp.concatenate([jnp.where(mine, do2, zero), extra], axis=1)
            t = lax.dot_general(dox, vx, NT, preferred_element_type=F32)
            e = ds_ref[slot, sub]
            ds = (e.astype(F32) * t).astype(BF)
            dv.append(jnp.dot(do_t[sub * HEAD_DIM : (sub + 1) * HEAD_DIM], e, preferred_element_type=F32))
            ds_ref[slot, sub] = ds
            dk.append(jnp.dot(q_t[sub * HEAD_DIM : (sub + 1) * HEAD_DIM], ds, preferred_element_type=F32))
            dq.append(jnp.dot(ds, k2, preferred_element_type=F32))
        joined = jnp.concatenate(
            [
                jnp.where(low, dq[0], dq[1]).astype(BF),
                jnp.concatenate(dk, axis=0).T.astype(BF),
                jnp.concatenate(dv, axis=0).T.astype(BF),
            ],
            axis=1,
        )
        weights = jnp.concatenate([wall_ref[m] for m in range(3)], axis=1)
        dx_ref[...] += lax.dot_general(joined, weights, NT, preferred_element_type=F32)
        part = jnp.dot(nt_ref[...], joined, preferred_element_type=F32).astype(BF)
        part_ref[slot, :, :, :, : 3 * pw] = part.reshape(ranks, 2, chunk, 3 * pw)
        part = jnp.dot(gat_ref[...], ctx_ref[...], preferred_element_type=F32).astype(BF)
        part_ref[slot, :, :, :, 3 * pw :] = part.reshape(ranks, 2, chunk, pw)

    @pl.when(u >= 8)
    def _():
        blk = 16
        one, zero = jnp.ones((blk, slots), BF), jnp.zeros((blk, slots), BF)

        @pl.when(u == 8)
        def _():
            for copy in ins:
                copy.wait()

        def sub_block(c, carry):
            rows = pl.ds(pl.multiple_of((u - 8) * trows + c * blk, blk), blk)
            g = jnp.concatenate([ds_ref[s, sub, rows, :] for s in range(8) for sub in range(2)], axis=0)
            for t in range(3):
                ids = ids_ref[t, rows, :].astype(F32).astype(BF)
                hot = jnp.concatenate([jnp.where(ids == jnp.bfloat16(b), one, zero) for b in range(buckets)], axis=0)
                span = slice(t * buckets * blk, (t + 1) * buckets * blk)
                acc_ref[span, :] += lax.dot_general(hot, g, NT, preferred_element_type=F32)
            return carry

        lax.fori_loop(0, trows // blk, sub_block, 0)

    def event(step):
        return lambda body: pl.when(u == step)(body)

    def core_stage(i):
        core_out[i].wait_recv()
        for p in (opp, par):
            total = wide_f32(part_ref[4 + i, :, p]) + wide_f32(crecv_ref[i, :, p])
            part_ref[4 + i, :, p] = total.astype(BF)
        for r in order:
            far_out[i][0][r].start()

    def own_sides():
        for i in range(2):
            for r in order:
                far_out[i][1][r].start()

    def far_stage(i):
        core_out[2 + i].wait_recv()
        for r in order:
            far_out[i][0][r].wait_recv()
            k = rank ^ r
            total = wide_f32(part_ref[i, k, opp]) + wide_f32(crecv_ref[2 + i, k, opp]) + wide_f32(frecv_ref[i, k, opp])
            part_ref[i, k, opp] = total.astype(BF)
            xa_out[i][r].start()

    def side_stage(i, r):
        far_out[i][1][r].wait_recv()
        xa_out[i][r].wait_recv()
        k = rank ^ r
        total = wide_f32(part_ref[i, k, par]) + wide_f32(crecv_ref[2 + i, k, par])
        total = total + wide_f32(frecv_ref[i, k, par]) + wide_f32(xarecv_ref[i, r])
        part_ref[i, k, par] = total.astype(BF)
        if r & 1:
            za_out[i][r].start()

    def rank_stage(i, r):
        total = wide_f32(part_ref[i, rank ^ r, par])
        for k in feeds(r):
            za_out[i][k].wait_recv()
            total = total + wide_f32(zarecv_ref[i, k - 1])
        if r == 0:
            return total
        part_ref[i, rank ^ r, par] = total.astype(BF)
        za_out[i][r].start()

    def ffn_stage(r):
        for copy in xf_last if r == 0 else [xf_out[r]]:
            copy.wait_recv()
        total = wide_f32(fsum_ref[rank ^ r, par]) + wide_f32(xfrecv_ref[r])
        for k in feeds(r):
            zf_out[k].wait_recv()
            total = total + wide_f32(zfrecv_ref[k - 1])
        if r == 0:
            return total
        xfrecv_ref[r] = total.astype(BF)
        zf_out[r].start()

    def input_gradient():
        gm_in.wait()
        x = x_ref[...].astype(F32)
        inv = lax.rsqrt(jnp.mean(x * x, axis=-1, keepdims=True) + EPS)
        upstream = dx_ref[...]
        lifted = upstream * gain_ref[...].astype(F32)[None]
        inner = jnp.mean(lifted * x, axis=-1, keepdims=True)
        gi_ref[...] = gi_ref[...] + inv * lifted - x * (inv * inv * inv * inner)
        gains = jnp.sum(upstream * x * inv, axis=0, keepdims=True)
        lanes = d // LANES
        for r in range(4):
            for j in range(lanes):
                span = slice(j * LANES, (j + 1) * LANES)
                nsend_ref[r, 3 * buckets + j : 3 * buckets + j + 1, :] = gains[:, span]
                nsend_ref[r, 3 * buckets + lanes + j : 3 * buckets + lanes + j + 1, :] = gain2_ref[:, span]

    plan = [[] for _ in range(steps)]
    for i in range(2):
        plan[2 * i].append(core_out[i].start)
        plan[2 * i + 1].append(functools.partial(core_stage, i))
        plan[4 + i].append(core_out[2 + i].start)
    plan[3].append(own_sides)
    for k, r in enumerate(range(ranks - 1, 0, -1)):
        plan[(3, 6, 8)[k] if ranks == 4 else 3 + k * 6 // ranks].append(functools.partial(ffn_stage, r))
    plan[6].append(functools.partial(far_stage, 0))
    plan[7].append(input_gradient)
    plan[8].append(functools.partial(far_stage, 1))
    plan[8].append(xf_last[0].start)
    plan[12].extend(functools.partial(side_stage, 0, r) for r in order)
    plan[15].extend(functools.partial(rank_stage, 0, r) for r in range(ranks - 2, 0, -2))
    for k in range(steps):

        @pl.when(u == k)
        def _():
            for action in plan[k]:
                action()

    @pl.when(u == steps - 1)
    def _():
        blk, cols = 16, 16 * 16
        same = lax.broadcasted_iota(I32, (blk, cols), 0) == (lax.broadcasted_iota(I32, (blk, cols), 1) & (blk - 1))
        picked = [
            jnp.sum(jnp.where(same, acc_ref[b * blk : (b + 1) * blk, :], 0.0), axis=0, keepdims=True)
            for b in range(3 * buckets)
        ]
        picked = jnp.concatenate(picked, axis=0)
        source = lax.broadcasted_iota(I32, (cols, LANES), 0) >> 4
        target = lax.broadcasted_iota(I32, (cols, LANES), 1)
        for r in range(4):
            choose = jnp.where((source == target + heads * r) & (target < heads), 1.0, 0.0).astype(F32)
            nsend_ref[r, : 3 * buckets, :] = jnp.dot(
                picked, choose, preferred_element_type=F32, precision=lax.Precision.HIGHEST
            )
        for copy in sn_out + out_out[1:]:
            copy.start()

        def finish(i):
            total = rank_stage(i, 0)
            cols = slice(i * pw, (i + 1) * pw)
            gq_ref[:, cols] = total[:, :pw]
            gk_ref[:, cols] = total[:, pw : 2 * pw]
            gv_ref[:, cols] = total[:, 2 * pw : 3 * pw]
            go_ref[cols, :] = total[:, 3 * pw :].T

        for r in order[:-1]:
            side_stage(1, r)
        for copy in sn_out:
            copy.wait()
        nsend_ref[1] = nsend_ref[0] + nrecv_ref[0] + nrecv_ref[1] + nrecv_ref[2]
        sx_out.start()
        xf_last[1].start()
        side_stage(1, 0)
        finish(0)
        for r in range(ranks - 2, 0, -2):
            rank_stage(1, r)
        sx_out.wait()
        nsend_ref[2] = nsend_ref[1] + sxrecv_ref[...]
        for r in range(1, ranks):
            sz_out[r].start()
        total = ffn_stage(0)
        full, rest = split_quarter(ff)
        for m, ref in enumerate((fg_ref, fu_ref, fd_ref)):
            ref[:full, :] = total[:, m * full : (m + 1) * full].T
            if rest:
                ref[full:, :] = total[:, 3 * full + m * rest : 3 * full + (m + 1) * rest].T
        total = nsend_ref[2]
        for r in range(1, ranks):
            sz_out[r].wait_recv()
            total = total + szrecv_ref[r - 1]
        small_ref[...] = total
        finish(1)
        for copy in out_out:
            copy.wait()
        for i in range(2):
            for copy in far_out[i][0] + far_out[i][1] + xa_out[i] + za_out[i][1:]:
                copy.wait_send()
        for copy in core_out + xf_out[1:] + xf_last + zf_out[1:] + sz_out[1:]:
            copy.wait_send()


def backward(wide, buckets, ff, ga, x, gain, gain2, fsum, gm, e, ids, out, wo_all, ctx, linv, qkv, w_all, trows=64):
    slots, d = x.shape
    heads = 4
    pw = 2 * HEAD_DIM
    ranks, chunk = wide // 2, d // wide
    packed = fsum.shape[-1]
    width = heads * HEAD_DIM
    small = 3 * buckets + 2 * d // LANES
    vmem, anywhere = pl.BlockSpec(memory_space=pltpu.VMEM), pl.BlockSpec(memory_space=pl.ANY)
    shape = jax.ShapeDtypeStruct
    dma = pltpu.SemaphoreType.DMA

    def slot(u):
        return backward_slot(jnp.minimum(u, 7))

    return pl.pallas_call(
        functools.partial(backward_kernel, wide, heads, buckets, trows, ff),
        grid=(8 + slots // trows,),
        in_specs=[vmem] * 5 + [anywhere] * 6 + [
            pl.BlockSpec((pw, d), lambda u: (slot(u), 0)),
            pl.BlockSpec((slots, pw), lambda u: (0, slot(u))),
            pl.BlockSpec((slots, pw), lambda u: (0, slot(u))),
            pl.BlockSpec((3, slots, pw), lambda u: (0, 0, slot(u))),
            pl.BlockSpec((3, d, pw), lambda u: (0, 0, slot(u))),
        ],
        out_specs=[vmem, anywhere] + [vmem] * 8,
        out_shape=[
            shape((slots, d), F32),
            shape((slots, d), BF),
            shape((small, LANES), F32),
            shape((chunk, width), F32),
            shape((chunk, width), F32),
            shape((chunk, width), F32),
            shape((width, chunk), F32),
            shape((ff, chunk), F32),
            shape((ff, chunk), F32),
            shape((ff, chunk), F32),
        ],
        scratch_shapes=[
            pltpu.VMEM((8, 2, slots, slots), BF),
            pltpu.VMEM((3, slots, slots), I32),
            pltpu.VMEM((d, slots), BF),
            pltpu.VMEM((d, slots), BF),
            pltpu.VMEM((slots, d), F32),
            pltpu.VMEM((3 * buckets * 16, 16 * 16), F32),
            pltpu.VMEM((8, ranks, 2, chunk, 4 * pw), BF),
            pltpu.VMEM((4, ranks, 2, chunk, 4 * pw), BF),
            pltpu.VMEM((2, ranks, 2, chunk, 4 * pw), BF),
            pltpu.VMEM((2, ranks, chunk, 4 * pw), BF),
            pltpu.VMEM((2, ranks - 1, chunk, 4 * pw), BF),
            pltpu.VMEM((ranks, chunk, packed), BF),
            pltpu.VMEM((ranks - 1, chunk, packed), BF),
            pltpu.VMEM((4, small, LANES), F32),
            pltpu.VMEM((3, small, LANES), F32),
            pltpu.VMEM((small, LANES), F32),
            pltpu.VMEM((ranks - 1, small, LANES), F32),
            dma((4,)), dma((2,)), dma((4, 2)), dma((2, 2, ranks, 2)), dma((2, 2)), dma((ranks + 1, 2)), dma((ranks - 1, 2)),
            dma((2, ranks, 2)), dma((2, ranks - 1, 2)), dma((3, 2)), dma((2,)), dma((ranks - 1, 2)),
        ],
        compiler_params=pltpu.CompilerParams(
            vmem_limit_bytes=VMEM_LIMIT, collective_id=3, has_side_effects=True
        ),
        cost_estimate=pl.CostEstimate(flops=30 * slots * d * d, bytes_accessed=60 << 20, transcendentals=0),
        name="backward",
    )(ga, x, gain, gain2, fsum, gm, e, *ids, out, wo_all, ctx, linv, qkv, w_all)


def results_kernel(
    wide, narrow, buckets, heads, middle_ref, out_ref, outin_ref, gi_ref, small_ref, *rest,
):
    sources, (block_ref, go_ref, ga_ref, gf_ref, tr_ref, th_ref, tv_ref), targets = rest[:7], rest[7:14], rest[14:]
    block_ref[...] = (middle_ref[...] + (out_ref[...].astype(F32) + outin_ref[...].astype(F32))).astype(BF)
    go_ref[...] = gi_ref[...]

    @pl.when(pl.program_id(0) == 0)
    def _():
        for a, b in zip(sources, targets):
            b[...] = a[...]
        w, n = lax.axis_index("wide"), lax.axis_index("narrow")
        d = middle_ref.shape[1]
        per, own = d // (wide * narrow), buckets // wide
        start = (w * narrow + n) * per
        for k, ref in enumerate((ga_ref, gf_ref)):
            row = small_ref[pl.ds(3 * buckets + k * (d // LANES) + start // LANES, 1), :]
            lane = lax.broadcasted_iota(I32, (per, LANES), 1)
            mine = lane == lax.broadcasted_iota(I32, (per, LANES), 0) + start % LANES
            ref[...] = jnp.sum(jnp.where(mine, jnp.broadcast_to(row, (per, LANES)), 0.0), axis=1)
        for k, ref in enumerate((tr_ref, th_ref, tv_ref)):
            ref[...] = small_ref[pl.ds(k * buckets + w * own, own), :heads]


def results(wide, narrow, buckets, heads, middle, out, outin, small, grad_input, big):
    slots, d = middle.shape
    shape = jax.ShapeDtypeStruct
    per, own = d // (wide * narrow), buckets // wide
    rows = pl.BlockSpec((slots // 4, d), lambda i: (i, 0))
    whole = lambda *sh: pl.BlockSpec(sh, lambda i: (0,) * len(sh))
    return pl.pallas_call(
        functools.partial(results_kernel, wide, narrow, buckets, heads),
        grid=(4,),
        in_specs=[rows] * 4 + [whole(*small.shape)] + [whole(*x.shape) for x in big],
        out_specs=[rows] * 2 + [whole(per)] * 2 + [whole(own, heads)] * 3 + [whole(*x.shape) for x in big],
        out_shape=[shape((slots, d), BF), shape((slots, d), F32)] + [shape((per,), F32)] * 2
        + [shape((own, heads), F32)] * 3 + [shape(x.shape, x.dtype) for x in big],
        compiler_params=pltpu.CompilerParams(vmem_limit_bytes=VMEM_LIMIT),
        name="results",
    )(middle, out, outin, grad_input, small, *big)


def shards(
    wide, narrow, hidden_in, grad_out, gain_attn, gain_ffn, w_query, w_key, w_value, w_output,
    table_rel, table_horiz, table_vert, wi_gate, wi_up, wo_ffn, counts, patch_mask,
    bucket_rel, bucket_horiz, bucket_vert,
):
    slots = bucket_rel.shape[1]
    rows, d = hidden_in.shape
    buckets, heads = table_rel.shape
    width = w_query.shape[1]
    ff = wi_gate.shape[1]
    assert rows == slots and narrow == 4 and wide >= 4 and heads * HEAD_DIM == width
    ids = (bucket_rel, bucket_horiz, bucket_vert)

    qkv, exps, context, linv, w_all, wo_all, middle, ffn_own, grad_far, wg_core, wu_core, wd_core = forward(
        counts, patch_mask, hidden_in, gain_attn, gain_ffn, (table_rel.T, table_horiz.T, table_vert.T),
        w_query, w_key, w_value, w_output, ids, grad_out, wi_gate.T, wi_up.T, wo_ffn,
    )
    out, ffn_sum, grad_middle, grad_attn, grad_gain_second = feed_forward(
        ffn_own, grad_out, grad_far, middle, gain_ffn,
        (wi_gate.T, wi_up.T, wo_ffn), (wg_core, wu_core, wd_core),
    )
    grad_input, out_in, small, gq, gk, gv, go, fg, fu, fd = backward(
        wide, buckets, ff, grad_attn, hidden_in, gain_attn, grad_gain_second,
        ffn_sum.reshape(wide // 2, 2, d // wide, -1), grad_middle, exps, ids, out,
        wo_all, context, linv, qkv, w_all,
    )
    block_out, grad_input, gain1, gain2, rel, horiz, vert, gq, gk, gv, go, fg, fu, fd = results(
        wide, narrow, buckets, heads, middle, out, out_in, small, grad_input, (gq, gk, gv, go, fg, fu, fd)
    )
    return (
        block_out, grad_input, gain1, gain2, gq, gk, gv, go, rel, horiz, vert, fg.T, fu.T, fd,
    )


def solution(mesh):
    rows, both = P(("wide", "narrow"), None), P(("wide", "narrow"))
    cols, across = P(None, "narrow"), P("narrow", None)
    grid, turned = P("wide", "narrow"), P("narrow", "wide")
    pages = P("wide", None, None)
    return jax.shard_map(
        functools.partial(shards, mesh.shape["wide"], mesh.shape["narrow"]),
        mesh=mesh,
        in_specs=(
            rows, rows, P(), P(), cols, cols, cols, across, cols, cols, cols, cols, cols, across,
            P("wide"), P("wide", None), pages, pages, pages,
        ),
        out_specs=(
            rows, rows, both, both, grid, grid, grid, turned, grid, grid, grid, grid, grid, turned,
        ),
        check_vma=False,
    )
```

time: 249 us -> 206 us (0.83)
  Pallas kernels: 229 us -> 205 us
  local copies, waits for them, and re-layouts: 10.1 us -> 0 us
  other arithmetic: 8.43 us -> 0 us
    pallas_call x1, Pallas kernels: 115 us -> 96.2 us  [backward(): pl.pallas_call(functools.partial(backward_kernel, wide, heads, buckets, t...]
    unnamed x26 -> x0, local copies, waits for them, and re-layouts: 6.18 us -> none
    pallas_call x2 -> x3, Pallas kernels: 114 us -> 109 us  [the longest x1 53.6 us: feed_forward(): pl.pallas_call(functools.partial(ffn_kernel, block, ff), in_specs=[anywhe...]
    convert_element_type x2 -> x0, other arithmetic: 3.81 us -> none  [the longest x1 3.8 us: shards(): (middle + (out[:slots].astype(F32) + out_in.astype(F32))).astype(BF)]
    broadcast_in_dim x2 -> x0, other arithmetic: 2.55 us -> none  [the longest x1 1.27 us: shards(): gain_first[None]]
where the time goes in v1:
time: 206 us
  Pallas kernels  205 us (100%)
    pallas_call x1, Pallas kernels, backward(): pl.pallas_call(functools.partial(backward_kernel, wide, heads, buckets, t...  96.2 us
    pallas_call x1, Pallas kernels, feed_forward(): pl.pallas_call(functools.partial(ffn_kernel, block, ff), in_specs=[anywhe...  53.6 us
    pallas_call x1, Pallas kernels, forward(): pl.pallas_call(functools.partial(forward_kernel, heads, buckets, chunk),...  49 us
    pallas_call x1, Pallas kernels, results(): pl.pallas_call(functools.partial(results_kernel, wide, narrow, buckets, h...  6.2 us

profile of v1, /device:TPU:0, one launch (start us, length us, event | category | flops | bytes accessed | tf_op | source)
XLA Modules:
  0.0 205.9 jit_solution(13840348830137865353)
XLA Ops:
  0.6 49.0 %forward.1 = (bf16[3,512,1024]{2,1,0:T(8,128)(2,1)}, bf16[8,2,512,512]{3,2,1,0:T(8,128)(2,1)}, bf16[512,1024]{1,0:T(8,128)(2,1)}, f32[512,1024]{1,0:T(8,128)}, b...) custom-call(s32[4]{0:T(128)} %counts_ref.1, ...), custom_call_target="tpu_custom_call" | custom-call | flops 10737418240 | bytes 41943040 | tf_op jit(solution)/shard_map/forward/pallas_call | solution.py:272
  49.7 53.6 %feed_forward.1 = (bf16[1024,1024]{1,0:T(8,128)(2,1)}, bf16[1024,2176]{1,0:T(8,128)(2,1)}, f32[512,1024]{1,0:T(8,128)}, bf16[512,1024]{1,0:T(8,128)(2,1)}, f32[1,1024]{1,0:T(1,128)}) custom-call(bf16[512,1024]{1,0:T(8,128)(2,1)} %get-tuple-element.56.x_ref, bf16[512,1024]{1,0:T(8,128)(2,1)} %go_ref.3, bf16[512,1024]{1,0:T(8,128)(2,1)} %get-tuple-element.57.gofar_ref, ...), custom_call_target="tpu_custom_call" | custom-call | flops 13287555072 | bytes 41943040 | tf_op jit(solution)/shard_map/feed_forward/pallas_call | solution.py:459
  103.3 96.2 %backward.1 = (f32[512,1024]{1,0:T(8,128)}, bf16[512,1024]{1,0:T(8,128)(2,1)}, f32[112,128]{1,0:T(8,128)}, f32[128,256]{1,0:T(8,128)}, f32[128,256]{1,0:T(8,128)...) custom-call(bf16[512,1024]{1,0:T(8,128)(2,1)} %get-tuple-element.62., ...), custom_call_target="tpu_custom_call" | custom-call | flops 16106127360 | bytes 62914560 | tf_op jit(solution)/shard_map/backward/pallas_call | solution.py:835
  199.5 6.2 %results.1 = (bf16[512,1024]{1,0:T(8,128)(2,1)}, f32[512,1024]{1,0:T(8,128)}, f32[32]{0:T(128)}, f32[32]{0:T(128)}, f32[4,4]{1,0:T(4,128)}, /*index=5*/f32[4,4]{...) custom-call(f32[512,1024]{1,0:T(8,128)} %get-tuple-element.55.middle, ...), custom_call_target="tpu_custom_call" | custom-call | tf_op jit(solution)/shard_map/results/pallas_call | solution.py:917

commit v2 on v1

--- a/solution.py
+++ b/solution.py
@@ -49,9 +49,9 @@
     heads, buckets, chunk,
     counts_ref, patch_ref, x_ref, gain1_ref, gain2_ref, tr_ref, th_ref, tv_ref,
     wq_ref, wk_ref, wv_ref, wo_ref, ir_ref, ih_ref, iv_ref, go_ref, wg_ref, wu_ref, wd_ref,
-    qkv_ref, e_ref, ctx_ref, linv_ref, wall_ref, woall_ref, middle_ref, ffn_ref, gofar_ref, wgc_ref, wuc_ref, wdc_ref,
-    normed_ref, mask_ref, ids_ref, tab_ref, tabs_ref, words_ref, ebuf_ref,
-    own_sem, id_sem, e_sem, core_sem, far_sem, deep_sem, wide_sem, fwd_sem, tab_sem, big_sem,
+    qkv_to, e_ref, ctx_to, linv_to, wall_to, woall_to, middle_ref, ffn_ref, gofar_ref, wgc_ref, wuc_ref, wdc_ref,
+    qkv_ref, ctx_ref, linv_ref, wall_ref, woall_ref, normed_ref, mask_ref, ids_ref, tab_ref, tabs_ref, words_ref, ebuf_ref,
+    own_sem, id_sem, e_sem, core_sem, far_sem, deep_sem, wide_sem, fwd_sem, tab_sem, big_sem, leave_sem,
 ):
     pw = 2 * HEAD_DIM
     slots, d = x_ref.shape
@@ -136,6 +136,16 @@
 
     def e_out(parity, slot):
         return pltpu.make_async_copy(ebuf_ref.at[parity], e_ref.at[slot], e_sem.at[parity])
+
+    def leaving(slot):
+        cols = pl.ds(pl.multiple_of(slot * pw, pw), pw)
+        pairs = (
+            (wall_ref.at[:, :, cols], wall_to.at[:, :, cols]),
+            (qkv_ref.at[:, :, cols], qkv_to.at[:, :, cols]),
+            (ctx_ref.at[:, cols], ctx_to.at[:, cols]),
+            (linv_ref.at[:, cols], linv_to.at[:, cols]),
+        )
+        return [pltpu.make_async_copy(a, b, leave_sem.at[k, slot]) for k, (a, b) in enumerate(pairs)]
 
     def slot_of(t):
         late = 4 + 2 * (t & 1) + jnp.where(t >= 6, other, half)
@@ -236,6 +246,8 @@
             linv_ref[rows, cols] = linv
             ctx_ref[rows, cols] = (jnp.where(low, outs[0][:, :pw], outs[1][:, :pw]) * linv).astype(BF)
         e_out(parity, slot).start()
+        for copy in leaving(slot):
+            copy.start()
         return carry
 
     lax.fori_loop(0, 8, step, 0)
@@ -244,6 +256,8 @@
         core_out[p][3].wait_recv()
     for copy in fwd_out[3] + last_out[3:]:
         copy.wait_recv()
+    wo_leaving = pltpu.make_async_copy(woall_ref, woall_to, id_sem.at[0])
+    wo_leaving.start()
     middle = x_ref[...].astype(F32) + jnp.dot(ctx_ref[...], woall_ref[...], preferred_element_type=F32)
     middle_ref[...] = middle
     inv = lax.rsqrt(jnp.mean(middle * middle, axis=-1, keepdims=True) + EPS)
@@ -257,6 +271,10 @@
             copy.wait_send()
     for copy in ffn_out:
         copy.wait()
+    for slot in range(8):
+        for copy in leaving(slot):
+            copy.wait()
+    wo_leaving.wait()
     go_out.wait()
 
 
@@ -272,7 +290,7 @@
     return pl.pallas_call(
         functools.partial(forward_kernel, heads, buckets, chunk),
         in_specs=[pl.BlockSpec(memory_space=pltpu.SMEM)] + [vmem] * 7 + [anywhere] * 11,
-        out_specs=[vmem, anywhere] + [vmem] * 6 + [anywhere] * 4,
+        out_specs=[anywhere] * 6 + [vmem] * 2 + [anywhere] * 4,
         out_shape=[
             shape((3, slots, d), BF),
             shape((8, 2, slots, slots), BF),
@@ -288,6 +306,11 @@
             shape((ff, d), BF),
         ],
         scratch_shapes=[
+            pltpu.VMEM((3, slots, d), BF),
+            pltpu.VMEM((slots, d), BF),
+            pltpu.VMEM((slots, d), F32),
+            pltpu.VMEM((3, d, d), BF),
+            pltpu.VMEM((d, d), BF),
             pltpu.VMEM((slots, d), BF),
             pltpu.VMEM((slots, 2 * HEAD_DIM), BF),
             pltpu.VMEM((3, slots, slots), I32),
@@ -296,7 +319,7 @@
             pltpu.VMEM((8, 8, LANES), I32),
             pltpu.VMEM((2, 2, slots, slots), BF),
             dma((2, 4)), dma((3,)), dma((2,)), dma((2, 4, 2)), dma((4, 2)), dma((4, 2)), dma((4, 2, 2)), dma((4, 3, 2)),
-            dma((3, 2)), dma((4, 2)),
+            dma((3, 2)), dma((4, 2)), dma((4, 8)),
         ],
         compiler_params=pltpu.CompilerParams(
             vmem_limit_bytes=VMEM_LIMIT, collective_id=1, has_side_effects=True
@@ -327,9 +350,9 @@
 def ffn_kernel(
     block, ff,
     x_ref, go_ref, gofar_ref, middle_ref, gain_ref, w0_ref, w1_ref, w2_ref, c0_ref, c1_ref, c2_ref,
-    out_ref, sum_ref, gm_ref, ga_ref, gain_out_ref,
-    xall_ref, gall_ref, wgu_ref, wd_ref, xt_ref, gt_ref, act_ref, send_ref, recv_ref, own_ref, backfar_ref, backin_ref,
-    in_sem, w_sem, x_sem, back_sem, dw_sem,
+    out_to, sum_to, gm_to, ga_to, gain_out_ref,
+    out_ref, sum_ref, gm_ref, ga_ref, xall_ref, gall_ref, wgu_ref, wd_ref, xt_ref, gt_ref, act_ref, send_ref, recv_ref, own_ref, backfar_ref, backin_ref,
+    in_sem, w_sem, x_sem, back_sem, dw_sem, leave_sem, end_sem,
 ):
     slots, d = middle_ref.shape
     halves = slots // block
@@ -404,6 +427,7 @@
                 back_out[i].start()
 
         out_ref[rows, :] = jnp.dot(hidden, wd_ref[...], preferred_element_type=F32).astype(BF)
+        pltpu.make_async_copy(out_ref.at[rows, :], out_to.at[rows, :], leave_sem.at[b]).start()
         return carry
 
     lax.fori_loop(0, 2 * halves, step, 0)
@@ -428,24 +452,39 @@
             if used < target.shape[1]:
                 target[rows, used:] = jnp.zeros((tile, target.shape[1] - used), BF)
         dw_out[c].start()
+    leaving = []
     for c in range(2):
         rows = slice(c * tile, (c + 1) * tile)
         dw_out[c].wait_recv()
         sum_ref[rows, :] = (sum_ref[rows, :].astype(F32) + recv_ref[rows, :].astype(F32)).astype(BF)
-
-    for copy in back_out:
-        copy.wait_recv()
-    middle = middle_ref[...]
-    inv = lax.rsqrt(jnp.mean(middle * middle, axis=-1, keepdims=True) + EPS)
-    upstream = own_ref[...] + backin_ref[...].astype(F32)
-    lifted = upstream * gain_ref[...].astype(F32)[None]
-    inner = jnp.mean(lifted * middle, axis=-1, keepdims=True)
-    gain_out_ref[...] = jnp.sum(upstream * middle * inv, axis=0, keepdims=True)
-    gm = gall_ref[0:slots, :].astype(F32) + inv * lifted - middle * (inv * inv * inv * inner)
-    gm_ref[...] = gm
-    ga_ref[...] = gm.astype(BF)
+        at = pl.ds(c * tile, tile)
+        leaving.append(pltpu.make_async_copy(sum_ref.at[at, :], sum_to.at[at, :], end_sem.at[c]))
+        leaving[-1].start()
+
+    gains = 0.0
+    for i in range(halves):
+        rows, at = slice(i * block, (i + 1) * block), pl.ds(i * block, block)
+        back_out[i].wait_recv()
+        middle = middle_ref[rows, :]
+        inv = lax.rsqrt(jnp.mean(middle * middle, axis=-1, keepdims=True) + EPS)
+        upstream = own_ref[rows, :] + backin_ref[rows, :].astype(F32)
+        lifted = upstream * gain_ref[...].astype(F32)[None]
+        inner = jnp.mean(lifted * middle, axis=-1, keepdims=True)
+        gains = gains + jnp.sum(upstream * middle * inv, axis=0, keepdims=True)
+        gm = gall_ref[rows, :].astype(F32) + inv * lifted - middle * (inv * inv * inv * inner)
+        gm_ref[rows, :] = gm
+        ga_ref[rows, :] = gm.astype(BF)
+        for k, (a, b) in enumerate(((gm_ref, gm_to), (ga_ref, ga_to))):
+            leaving.append(pltpu.make_async_copy(a.at[at, :], b.at[at, :], end_sem.at[2 + 2 * i + k]))
+            leaving[-1].start()
+    gain_out_ref[...] = gains
     for copy in x_out + back_out + dw_out:
         copy.wait_send()
+    for b in range(2 * halves):
+        at = pl.ds(b * block, block)
+        pltpu.make_async_copy(out_ref.at[at, :], out_to.at[at, :], leave_sem.at[b]).wait()
+    for copy in leaving:
+        copy.wait()
 
 
 def feed_forward(x, go, gofar, middle, gain, own, other, block=256):
@@ -459,7 +498,7 @@
     return pl.pallas_call(
         functools.partial(ffn_kernel, block, ff),
         in_specs=[anywhere] * 3 + [vmem] * 2 + [anywhere] * 6,
-        out_specs=[vmem] * 5,
+        out_specs=[anywhere] * 4 + [vmem],
         out_shape=[
             shape((2 * slots, d), BF),
             shape((d, packed), BF),
@@ -468,6 +507,10 @@
             shape((1, d), F32),
         ],
         scratch_shapes=[
+            pltpu.VMEM((2 * slots, d), BF),
+            pltpu.VMEM((d, packed), BF),
+            pltpu.VMEM((slots, d), F32),
+            pltpu.VMEM((slots, d), BF),
             pltpu.VMEM((2 * slots, d), BF),
             pltpu.VMEM((2 * slots, d), BF),
             pltpu.VMEM((4 * ff, d), BF),
@@ -481,6 +524,7 @@
             pltpu.VMEM((slots, d), BF),
             pltpu.VMEM((slots, d), BF),
             dma((3,)), dma((3, 2, 2)), dma((halves, 2)), dma((halves, 2)), dma((2, 2)),
+            dma((2 * halves,)), dma((2 + 2 * halves,)),
         ],
         compiler_params=pltpu.CompilerParams(
             vmem_limit_bytes=VMEM_LIMIT, collective_id=2, has_side_effects=True
@@ -499,7 +543,7 @@
     ga_ref, x_ref, gain_ref, gain2_ref, fsum_ref, gm_ref, e_ref, ir_ref, ih_ref, iv_ref, out_ref,
     wo_ref, ctx_ref, linv_ref, qkv_ref, wall_ref,
     gi_ref, outin_ref, small_ref, gq_ref, gk_ref, gv_ref, go_ref, fg_ref, fu_ref, fd_ref,
-    ds_ref, ids_ref, nt_ref, gat_ref, dx_ref, acc_ref, part_ref, crecv_ref, frecv_ref, xarecv_ref, zarecv_ref,
+    gib_ref, fown_ref, ds_ref, ids_ref, nt_ref, gat_ref, dx_ref, acc_ref, part_ref, crecv_ref, frecv_ref, xarecv_ref, zarecv_ref,
     xfrecv_ref, zfrecv_ref, nsend_ref, nrecv_ref, sxrecv_ref, szrecv_ref,
     in_sem, e_sem, core_sem, far_sem, out_sem, xf_sem, zf_sem, xa_sem, za_sem, sn_sem, sx_sem, sz_sem,
 ):
@@ -518,7 +562,9 @@
     slot = slot_of(jnp.minimum(u, 7))
 
     ins = [pltpu.make_async_copy(r.at[n], ids_ref.at[t], in_sem.at[t]) for t, r in enumerate((ir_ref, ih_ref, iv_ref))]
-    gm_in = pltpu.make_async_copy(gm_ref, gi_ref, in_sem.at[3])
+    gm_in = pltpu.make_async_copy(gm_ref, gib_ref, in_sem.at[3])
+    fown_in = pltpu.make_async_copy(fsum_ref.at[:, par], fown_ref, in_sem.at[4])
+    gi_out = pltpu.make_async_copy(gib_ref, gi_ref, in_sem.at[5])
     core_out = [remote(part_ref.at[s], crecv_ref.at[i], core_sem.at[i], core) for i, s in enumerate((6, 7, 2, 3))]
     order = list(range(ranks - 1, 0, -2)) + list(range(ranks - 2, -1, -2))
     far_out = [
@@ -570,6 +616,11 @@
     sx_out = remote(nsend_ref.at[1], sxrecv_ref, sx_sem, side)
     sz_out = [None] + [remote(nsend_ref.at[2], szrecv_ref.at[r - 1], sz_sem.at[r - 1], peer(r)) for r in range(1, ranks)]
 
+    def at_edge(end, middle):
+        edge = ((rank ^ (rank >> 1)) & 1) == 0
+        pl.when(edge)(lambda: end())
+        pl.when(jnp.logical_not(edge))(lambda: middle())
+
     def e_in(k):
         s = slot_of(k)
         return pltpu.make_async_copy(e_ref.at[s], ds_ref.at[s], e_sem.at[k & 1])
@@ -580,11 +631,16 @@
     @pl.when(u == 0)
     def _():
         e_in(0).start()
-        for copy in ins + [gm_in]:
+        for copy in [fown_in] + ins + [gm_in]:
             copy.start()
         greet([core, far, diag, side] + [peer(r) for r in range(1, ranks)])
-        for r in range(ranks - 1, 0, -1):
-            xf_out[r].start()
+        if ranks == 4:
+            xf_out[3].start()
+            at_edge(xf_out[1].start, xf_out[2].start)
+            at_edge(xf_out[2].start, xf_out[1].start)
+        else:
+            for r in range(ranks - 1, 0, -1):
+                xf_out[r].start()
         out_out[0].start()
         x = x_ref[...].astype(F32)
         inv = lax.rsqrt(jnp.mean(x * x, axis=-1, keepdims=True) + EPS)
@@ -708,7 +764,7 @@
     def ffn_stage(r):
         for copy in xf_last if r == 0 else [xf_out[r]]:
             copy.wait_recv()
-        total = wide_f32(fsum_ref[rank ^ r, par]) + wide_f32(xfrecv_ref[r])
+        total = wide_f32(fown_ref[rank ^ r]) + wide_f32(xfrecv_ref[r])
         for k in feeds(r):
             zf_out[k].wait_recv()
             total = total + wide_f32(zfrecv_ref[k - 1])
@@ -724,7 +780,8 @@
         upstream = dx_ref[...]
         lifted = upstream * gain_ref[...].astype(F32)[None]
         inner = jnp.mean(lifted * x, axis=-1, keepdims=True)
-        gi_ref[...] = gi_ref[...] + inv * lifted - x * (inv * inv * inv * inner)
+        gib_ref[...] = gib_ref[...] + inv * lifted - x * (inv * inv * inv * inner)
+        gi_out.start()
         gains = jnp.sum(upstream * x * inv, axis=0, keepdims=True)
         lanes = d // LANES
         for r in range(4):
@@ -739,8 +796,15 @@
         plan[2 * i + 1].append(functools.partial(core_stage, i))
         plan[4 + i].append(core_out[2 + i].start)
     plan[3].append(own_sides)
-    for k, r in enumerate(range(ranks - 1, 0, -1)):
-        plan[(3, 6, 8)[k] if ranks == 4 else 3 + k * 6 // ranks].append(functools.partial(ffn_stage, r))
+    plan[1].append(fown_in.wait)
+    if ranks == 4:
+        turn = lambda a, b: functools.partial(at_edge, functools.partial(ffn_stage, a), functools.partial(ffn_stage, b))
+        plan[2].append(functools.partial(ffn_stage, 3))
+        plan[5].append(turn(1, 2))
+        plan[8].append(turn(2, 1))
+    else:
+        for k, r in enumerate(range(ranks - 1, 0, -1)):
+            plan[3 + k * 6 // ranks].append(functools.partial(ffn_stage, r))
     plan[6].append(functools.partial(far_stage, 0))
     plan[7].append(input_gradient)
     plan[8].append(functools.partial(far_stage, 1))
@@ -808,6 +872,7 @@
             total = total + szrecv_ref[r - 1]
         small_ref[...] = total
         finish(1)
+        gi_out.wait()
         for copy in out_out:
             copy.wait()
         for i in range(2):
@@ -835,14 +900,14 @@
     return pl.pallas_call(
         functools.partial(backward_kernel, wide, heads, buckets, trows, ff),
         grid=(8 + slots // trows,),
-        in_specs=[vmem] * 5 + [anywhere] * 6 + [
+        in_specs=[vmem] * 4 + [anywhere] * 7 + [
             pl.BlockSpec((pw, d), lambda u: (slot(u), 0)),
             pl.BlockSpec((slots, pw), lambda u: (0, slot(u))),
             pl.BlockSpec((slots, pw), lambda u: (0, slot(u))),
             pl.BlockSpec((3, slots, pw), lambda u: (0, 0, slot(u))),
             pl.BlockSpec((3, d, pw), lambda u: (0, 0, slot(u))),
         ],
-        out_specs=[vmem, anywhere] + [vmem] * 8,
+        out_specs=[anywhere] * 2 + [vmem] * 8,
         out_shape=[
             shape((slots, d), F32),
             shape((slots, d), BF),
@@ -856,6 +921,8 @@
             shape((ff, chunk), F32),
         ],
         scratch_shapes=[
+            pltpu.VMEM((slots, d), F32),
+            pltpu.VMEM((ranks, chunk, packed), BF),
             pltpu.VMEM((8, 2, slots, slots), BF),
             pltpu.VMEM((3, slots, slots), I32),
             pltpu.VMEM((d, slots), BF),
@@ -873,7 +940,7 @@
             pltpu.VMEM((3, small, LANES), F32),
             pltpu.VMEM((small, LANES), F32),
             pltpu.VMEM((ranks - 1, small, LANES), F32),
-            dma((4,)), dma((2,)), dma((4, 2)), dma((2, 2, ranks, 2)), dma((2, 2)), dma((ranks + 1, 2)), dma((ranks - 1, 2)),
+            dma((6,)), dma((2,)), dma((4, 2)), dma((2, 2, ranks, 2)), dma((2, 2)), dma((ranks + 1, 2)), dma((ranks - 1, 2)),
             dma((2, ranks, 2)), dma((2, ranks - 1, 2)), dma((3, 2)), dma((2,)), dma((ranks - 1, 2)),
         ],
         compiler_params=pltpu.CompilerParams(

time: 206 us -> 188 us (0.913)
  Pallas kernels: 205 us -> 187 us
    pallas_call x1, Pallas kernels: 96.2 us -> 84.5 us  [backward(): pl.pallas_call(functools.partial(backward_kernel, wide, heads, buckets, t...]
    pallas_call x1, Pallas kernels: 49 us -> 44.9 us  [forward(): pl.pallas_call(functools.partial(forward_kernel, heads, buckets, chunk),...]
    pallas_call x1, Pallas kernels: 53.6 us -> 51 us  [feed_forward(): pl.pallas_call(functools.partial(ffn_kernel, block, ff), in_specs=[anywhe...]
where the time goes in v2:
time: 188 us; the launch traced here: 187 us
  Pallas kernels  187 us (99%)
    pallas_call x1, Pallas kernels, backward(): pl.pallas_call(functools.partial(backward_kernel, wide, heads, buckets, t...  84.5 us
    pallas_call x1, Pallas kernels, feed_forward(): pl.pallas_call(functools.partial(ffn_kernel, block, ff), in_specs=[anywhe...  51 us
    pallas_call x1, Pallas kernels, forward(): pl.pallas_call(functools.partial(forward_kernel, heads, buckets, chunk),...  44.9 us
    pallas_call x1, Pallas kernels, results(): pl.pallas_call(functools.partial(results_kernel, wide, narrow, buckets, h...  6.2 us

profile of v2, /device:TPU:0, one launch (start us, length us, event | category | flops | bytes accessed | tf_op | source)
XLA Modules:
  0.0 187.5 jit_solution(459426611626628985)
XLA Ops:
  0.6 44.9 %forward.1 = (bf16[3,512,1024]{2,1,0:T(8,128)(2,1)}, bf16[8,2,512,512]{3,2,1,0:T(8,128)(2,1)}, bf16[512,1024]{1,0:T(8,128)(2,1)}, f32[512,1024]{1,0:T(8,128)}, b...) custom-call(s32[4]{0:T(128)} %counts_ref.1, ...), custom_call_target="tpu_custom_call" | custom-call | flops 10737418240 | bytes 41943040 | tf_op jit(solution)/shard_map/forward/pallas_call | solution.py:290
  45.6 51.0 %feed_forward.1 = (bf16[1024,1024]{1,0:T(8,128)(2,1)}, bf16[1024,2176]{1,0:T(8,128)(2,1)}, f32[512,1024]{1,0:T(8,128)}, bf16[512,1024]{1,0:T(8,128)(2,1)}, f32[1,1024]{1,0:T(1,128)}) custom-call(bf16[512,1024]{1,0:T(8,128)(2,1)} %get-tuple-element.56.x_ref, bf16[512,1024]{1,0:T(8,128)(2,1)} %go_ref.3, bf16[512,1024]{1,0:T(8,128)(2,1)} %get-tuple-element.57.gofar_ref, ...), custom_call_target="tpu_custom_call" | custom-call | flops 13287555072 | bytes 41943040 | tf_op jit(solution)/shard_map/feed_forward/pallas_call | solution.py:498
  96.6 84.5 %backward.1 = (f32[512,1024]{1,0:T(8,128)}, bf16[512,1024]{1,0:T(8,128)(2,1)}, f32[112,128]{1,0:T(8,128)}, f32[128,256]{1,0:T(8,128)}, f32[128,256]{1,0:T(8,128)...) custom-call(bf16[512,1024]{1,0:T(8,128)(2,1)} %get-tuple-element.62., ...), custom_call_target="tpu_custom_call" | custom-call | flops 16106127360 | bytes 62914560 | tf_op jit(solution)/shard_map/backward/pallas_call | solution.py:900
  181.1 6.2 %results.1 = (bf16[512,1024]{1,0:T(8,128)(2,1)}, f32[512,1024]{1,0:T(8,128)}, f32[32]{0:T(128)}, f32[32]{0:T(128)}, f32[4,4]{1,0:T(4,128)}, /*index=5*/f32[4,4]{...) custom-call(f32[512,1024]{1,0:T(8,128)} %get-tuple-element.55.middle, ...), custom_call_target="tpu_custom_call" | custom-call | tf_op jit(solution)/shard_map/results/pallas_call | solution.py:984

commit v3 on v2

--- a/solution.py
+++ b/solution.py
@@ -544,8 +544,8 @@
     wo_ref, ctx_ref, linv_ref, qkv_ref, wall_ref,
     gi_ref, outin_ref, small_ref, gq_ref, gk_ref, gv_ref, go_ref, fg_ref, fu_ref, fd_ref,
     gib_ref, fown_ref, ds_ref, ids_ref, nt_ref, gat_ref, dx_ref, acc_ref, part_ref, crecv_ref, frecv_ref, xarecv_ref, zarecv_ref,
-    xfrecv_ref, zfrecv_ref, nsend_ref, nrecv_ref, sxrecv_ref, szrecv_ref,
-    in_sem, e_sem, core_sem, far_sem, out_sem, xf_sem, zf_sem, xa_sem, za_sem, sn_sem, sx_sem, sz_sem,
+    xfrecv_ref, zfrecv_ref, nsend_ref, nrecv_ref, parts_ref, srecv_ref,
+    in_sem, e_sem, core_sem, far_sem, out_sem, xf_sem, zf_sem, xa_sem, za_sem, sn_sem, ss_sem,
 ):
     pw = 2 * HEAD_DIM
     slots, d = ga_ref.shape
@@ -613,8 +613,9 @@
     sn_out = [
         remote(nsend_ref.at[r], nrecv_ref.at[r - 1], sn_sem.at[r - 1], dev) for r, dev in ((1, core), (2, far), (3, diag))
     ]
-    sx_out = remote(nsend_ref.at[1], sxrecv_ref, sx_sem, side)
-    sz_out = [None] + [remote(nsend_ref.at[2], szrecv_ref.at[r - 1], sz_sem.at[r - 1], peer(r)) for r in range(1, ranks)]
+    ss_out = [None] + [
+        remote(parts_ref.at[w ^ k], srecv_ref.at[k - 1], ss_sem.at[k - 1], (w ^ k, n)) for k in range(1, wide)
+    ]
 
     def at_edge(end, middle):
         edge = ((rank ^ (rank >> 1)) & 1) == 0
@@ -633,7 +634,7 @@
         e_in(0).start()
         for copy in [fown_in] + ins + [gm_in]:
             copy.start()
-        greet([core, far, diag, side] + [peer(r) for r in range(1, ranks)])
+        greet([core, far, diag] + [(w ^ k, n) for k in range(1, wide)])
         if ranks == 4:
             xf_out[3].start()
             at_edge(xf_out[1].start, xf_out[2].start)
@@ -648,6 +649,7 @@
         gat_ref[...] = ga_ref[...].T
         dx_ref[...] = jnp.zeros_like(dx_ref)
         acc_ref[...] = jnp.zeros_like(acc_ref)
+        parts_ref[...] = jnp.zeros_like(parts_ref)
 
     @pl.when(u < 8)
     def _():
@@ -697,24 +699,32 @@
     @pl.when(u >= 8)
     def _():
         blk = 16
-        one, zero = jnp.ones((blk, slots), BF), jnp.zeros((blk, slots), BF)
+        one, zero = jnp.ones((blk, 4 * slots), BF), jnp.zeros((blk, 4 * slots), BF)
 
         @pl.when(u == 8)
         def _():
             for copy in ins:
                 copy.wait()
 
+        group = 4
+
         def sub_block(c, carry):
-            rows = pl.ds(pl.multiple_of((u - 8) * trows + c * blk, blk), blk)
-            g = jnp.concatenate([ds_ref[s, sub, rows, :] for s in range(8) for sub in range(2)], axis=0)
+            starts = [pl.multiple_of((u - 8) * trows + (c * group + k) * blk, blk) for k in range(group)]
+            g = jnp.concatenate(
+                [
+                    jnp.concatenate([ds_ref[s, sub, pl.ds(at, blk), :] for s in range(8) for sub in range(2)], axis=0)
+                    for at in starts
+                ],
+                axis=1,
+            )
             for t in range(3):
-                ids = ids_ref[t, rows, :].astype(F32).astype(BF)
+                ids = jnp.concatenate([ids_ref[t, pl.ds(at, blk), :].astype(F32).astype(BF) for at in starts], axis=1)
                 hot = jnp.concatenate([jnp.where(ids == jnp.bfloat16(b), one, zero) for b in range(buckets)], axis=0)
                 span = slice(t * buckets * blk, (t + 1) * buckets * blk)
                 acc_ref[span, :] += lax.dot_general(hot, g, NT, preferred_element_type=F32)
             return carry
 
-        lax.fori_loop(0, trows // blk, sub_block, 0)
+        lax.fori_loop(0, trows // (blk * group), sub_block, 0)
 
     def event(step):
         return lambda body: pl.when(u == step)(body)
@@ -829,11 +839,10 @@
         picked = jnp.concatenate(picked, axis=0)
         source = lax.broadcasted_iota(I32, (cols, LANES), 0) >> 4
         target = lax.broadcasted_iota(I32, (cols, LANES), 1)
+        choose = jnp.where(source == target, 1.0, 0.0).astype(F32)
+        sums = jnp.dot(picked, choose, preferred_element_type=F32, precision=lax.Precision.HIGHEST)
         for r in range(4):
-            choose = jnp.where((source == target + heads * r) & (target < heads), 1.0, 0.0).astype(F32)
-            nsend_ref[r, : 3 * buckets, :] = jnp.dot(
-                picked, choose, preferred_element_type=F32, precision=lax.Precision.HIGHEST
-            )
+            nsend_ref[r, : 3 * buckets, :] = pltpu.roll(sums, LANES - heads * r, 1) if r else sums
         for copy in sn_out + out_out[1:]:
             copy.start()
 
@@ -850,26 +859,31 @@
         for copy in sn_out:
             copy.wait()
         nsend_ref[1] = nsend_ref[0] + nrecv_ref[0] + nrecv_ref[1] + nrecv_ref[2]
-        sx_out.start()
+        lanes, own = d // LANES, buckets // wide
+        for k in range(wide):
+            row = 3 * buckets + k * d // wide // LANES
+            parts_ref[k, 0:1, :] = nsend_ref[1, row : row + 1, :]
+            parts_ref[k, 1:2, :] = nsend_ref[1, row + lanes : row + lanes + 1, :]
+            for t in range(3):
+                at = t * buckets + k * own
+                parts_ref[k, 2 + t * own : 2 + (t + 1) * own, :] = nsend_ref[1, at : at + own, :]
+        for copy in ss_out[1:]:
+            copy.start()
         xf_last[1].start()
         side_stage(1, 0)
         finish(0)
         for r in range(ranks - 2, 0, -2):
             rank_stage(1, r)
-        sx_out.wait()
-        nsend_ref[2] = nsend_ref[1] + sxrecv_ref[...]
-        for r in range(1, ranks):
-            sz_out[r].start()
         total = ffn_stage(0)
         full, rest = split_quarter(ff)
         for m, ref in enumerate((fg_ref, fu_ref, fd_ref)):
             ref[:full, :] = total[:, m * full : (m + 1) * full].T
             if rest:
                 ref[full:, :] = total[:, 3 * full + m * rest : 3 * full + (m + 1) * rest].T
-        total = nsend_ref[2]
-        for r in range(1, ranks):
-            sz_out[r].wait_recv()
-            total = total + szrecv_ref[r - 1]
+        total = parts_ref[w]
+        for k in range(1, wide):
+            ss_out[k].wait_recv()
+            total = total + srecv_ref[k - 1]
         small_ref[...] = total
         finish(1)
         gi_out.wait()
@@ -878,7 +892,7 @@
         for i in range(2):
             for copy in far_out[i][0] + far_out[i][1] + xa_out[i] + za_out[i][1:]:
                 copy.wait_send()
-        for copy in core_out + xf_out[1:] + xf_last + zf_out[1:] + sz_out[1:]:
+        for copy in core_out + xf_out[1:] + xf_last + zf_out[1:] + ss_out[1:]:
             copy.wait_send()
 
 
@@ -890,6 +904,7 @@
     packed = fsum.shape[-1]
     width = heads * HEAD_DIM
     small = 3 * buckets + 2 * d // LANES
+    place = -(-(2 + 3 * (buckets // wide)) // 8) * 8
     vmem, anywhere = pl.BlockSpec(memory_space=pltpu.VMEM), pl.BlockSpec(memory_space=pl.ANY)
     shape = jax.ShapeDtypeStruct
     dma = pltpu.SemaphoreType.DMA
@@ -911,7 +926,7 @@
         out_shape=[
             shape((slots, d), F32),
             shape((slots, d), BF),
-            shape((small, LANES), F32),
+            shape((place, LANES), F32),
             shape((chunk, width), F32),
             shape((chunk, width), F32),
             shape((chunk, width), F32),
@@ -938,10 +953,10 @@
             pltpu.VMEM((ranks - 1, chunk, packed), BF),
             pltpu.VMEM((4, small, LANES), F32),
             pltpu.VMEM((3, small, LANES), F32),
-            pltpu.VMEM((small, LANES), F32),
-            pltpu.VMEM((ranks - 1, small, LANES), F32),
+            pltpu.VMEM((wide, place, LANES), F32),
+            pltpu.VMEM((wide - 1, place, LANES), F32),
             dma((6,)), dma((2,)), dma((4, 2)), dma((2, 2, ranks, 2)), dma((2, 2)), dma((ranks + 1, 2)), dma((ranks - 1, 2)),
-            dma((2, ranks, 2)), dma((2, ranks - 1, 2)), dma((3, 2)), dma((2,)), dma((ranks - 1, 2)),
+            dma((2, ranks, 2)), dma((2, ranks - 1, 2)), dma((3, 2)), dma((wide - 1, 2)),
         ],
         compiler_params=pltpu.CompilerParams(
             vmem_limit_bytes=VMEM_LIMIT, collective_id=3, has_side_effects=True
@@ -967,12 +982,12 @@
         per, own = d // (wide * narrow), buckets // wide
         start = (w * narrow + n) * per
         for k, ref in enumerate((ga_ref, gf_ref)):
-            row = small_ref[pl.ds(3 * buckets + k * (d // LANES) + start // LANES, 1), :]
+            row = small_ref[k : k + 1, :]
             lane = lax.broadcasted_iota(I32, (per, LANES), 1)
             mine = lane == lax.broadcasted_iota(I32, (per, LANES), 0) + start % LANES
             ref[...] = jnp.sum(jnp.where(mine, jnp.broadcast_to(row, (per, LANES)), 0.0), axis=1)
         for k, ref in enumerate((tr_ref, th_ref, tv_ref)):
-            ref[...] = small_ref[pl.ds(k * buckets + w * own, own), :heads]
+            ref[...] = small_ref[2 + k * own : 2 + (k + 1) * own, :heads]
 
 
 def results(wide, narrow, buckets, heads, middle, out, outin, small, grad_input, big):

time: 188 us -> 186 us (0.989)
  Pallas kernels: 187 us -> 185 us
    pallas_call x1, Pallas kernels: 84.5 us -> 82.4 us  [backward(): pl.pallas_call(functools.partial(backward_kernel, wide, heads, buckets, t...]
where the time goes in v3:
time: 186 us; the launch traced here: 185 us
  Pallas kernels  185 us (99%)
    pallas_call x1, Pallas kernels, backward(): pl.pallas_call(functools.partial(backward_kernel, wide, heads, buckets, t...  82.4 us
    pallas_call x1, Pallas kernels, feed_forward(): pl.pallas_call(functools.partial(ffn_kernel, block, ff), in_specs=[anywhe...  51 us
    pallas_call x1, Pallas kernels, forward(): pl.pallas_call(functools.partial(forward_kernel, heads, buckets, chunk),...  44.9 us
    pallas_call x1, Pallas kernels, results(): pl.pallas_call(functools.partial(results_kernel, wide, narrow, buckets, h...  6.18 us

profile of v3, /device:TPU:0, one launch (start us, length us, event | category | flops | bytes accessed | tf_op | source)
XLA Modules:
  0.0 185.4 jit_solution(1366768813954893503)
XLA Ops:
  0.6 44.9 %forward.1 = (bf16[3,512,1024]{2,1,0:T(8,128)(2,1)}, bf16[8,2,512,512]{3,2,1,0:T(8,128)(2,1)}, bf16[512,1024]{1,0:T(8,128)(2,1)}, f32[512,1024]{1,0:T(8,128)}, b...) custom-call(s32[4]{0:T(128)} %counts_ref.1, ...), custom_call_target="tpu_custom_call" | custom-call | flops 10737418240 | bytes 41943040 | tf_op jit(solution)/shard_map/forward/pallas_call | solution.py:290
  45.6 51.0 %feed_forward.1 = (bf16[1024,1024]{1,0:T(8,128)(2,1)}, bf16[1024,2176]{1,0:T(8,128)(2,1)}, f32[512,1024]{1,0:T(8,128)}, bf16[512,1024]{1,0:T(8,128)(2,1)}, f32[1,1024]{1,0:T(1,128)}) custom-call(bf16[512,1024]{1,0:T(8,128)(2,1)} %get-tuple-element.56.x_ref, bf16[512,1024]{1,0:T(8,128)(2,1)} %go_ref.3, bf16[512,1024]{1,0:T(8,128)(2,1)} %get-tuple-element.57.gofar_ref, ...), custom_call_target="tpu_custom_call" | custom-call | flops 13287555072 | bytes 41943040 | tf_op jit(solution)/shard_map/feed_forward/pallas_call | solution.py:498
  96.6 82.4 %backward.1 = (f32[512,1024]{1,0:T(8,128)}, bf16[512,1024]{1,0:T(8,128)(2,1)}, f32[16,128]{1,0:T(8,128)}, f32[128,256]{1,0:T(8,128)}, f32[128,256]{1,0:T(8,128)}...) custom-call(bf16[512,1024]{1,0:T(8,128)(2,1)} %get-tuple-element.62., ...), custom_call_target="tpu_custom_call" | custom-call | flops 16106127360 | bytes 62914560 | tf_op jit(solution)/shard_map/backward/pallas_call | solution.py:915
  179.0 6.2 %results.1 = (bf16[512,1024]{1,0:T(8,128)(2,1)}, f32[512,1024]{1,0:T(8,128)}, f32[32]{0:T(128)}, f32[32]{0:T(128)}, f32[4,4]{1,0:T(4,128)}, /*index=5*/f32[4,4]{...) custom-call(f32[512,1024]{1,0:T(8,128)} %get-tuple-element.55.middle, ...), custom_call_target="tpu_custom_call" | custom-call | tf_op jit(solution)/shard_map/results/pallas_call | solution.py:999

commit v4 on v3

--- a/solution.py
+++ b/solution.py
@@ -994,11 +994,11 @@
     slots, d = middle.shape
     shape = jax.ShapeDtypeStruct
     per, own = d // (wide * narrow), buckets // wide
-    rows = pl.BlockSpec((slots // 4, d), lambda i: (i, 0))
+    rows = pl.BlockSpec((slots // 2, d), lambda i: (i, 0))
     whole = lambda *sh: pl.BlockSpec(sh, lambda i: (0,) * len(sh))
     return pl.pallas_call(
         functools.partial(results_kernel, wide, narrow, buckets, heads),
-        grid=(4,),
+        grid=(2,),
         in_specs=[rows] * 4 + [whole(*small.shape)] + [whole(*x.shape) for x in big],
         out_specs=[rows] * 2 + [whole(per)] * 2 + [whole(own, heads)] * 3 + [whole(*x.shape) for x in big],
         out_shape=[shape((slots, d), BF), shape((slots, d), F32)] + [shape((per,), F32)] * 2

time: 186 us -> 185 us (level)
  no operation moved by 1% of the time
where the time goes in v4:
time: 185 us; the launch traced here: 184 us
  Pallas kernels  184 us (99%)
    pallas_call x1, Pallas kernels, backward(): pl.pallas_call(functools.partial(backward_kernel, wide, heads, buckets, t...  82.4 us
    pallas_call x1, Pallas kernels, feed_forward(): pl.pallas_call(functools.partial(ffn_kernel, block, ff), in_specs=[anywhe...  51 us
    pallas_call x1, Pallas kernels, forward(): pl.pallas_call(functools.partial(forward_kernel, heads, buckets, chunk),...  44.9 us
    pallas_call x1, Pallas kernels, results(): pl.pallas_call(functools.partial(results_kernel, wide, narrow, buckets, h...  5.22 us

profile of v4, /device:TPU:0, one launch (start us, length us, event | category | flops | bytes accessed | tf_op | source)
XLA Modules:
  0.0 184.4 jit_solution(6463145752586481625)
XLA Ops:
  0.6 44.9 %forward.1 = (bf16[3,512,1024]{2,1,0:T(8,128)(2,1)}, bf16[8,2,512,512]{3,2,1,0:T(8,128)(2,1)}, bf16[512,1024]{1,0:T(8,128)(2,1)}, f32[512,1024]{1,0:T(8,128)}, b...) custom-call(s32[4]{0:T(128)} %counts_ref.1, ...), custom_call_target="tpu_custom_call" | custom-call | flops 10737418240 | bytes 41943040 | tf_op jit(solution)/shard_map/forward/pallas_call | solution.py:290
  45.6 51.0 %feed_forward.1 = (bf16[1024,1024]{1,0:T(8,128)(2,1)}, bf16[1024,2176]{1,0:T(8,128)(2,1)}, f32[512,1024]{1,0:T(8,128)}, bf16[512,1024]{1,0:T(8,128)(2,1)}, f32[1,1024]{1,0:T(1,128)}) custom-call(bf16[512,1024]{1,0:T(8,128)(2,1)} %get-tuple-element.56.x_ref, bf16[512,1024]{1,0:T(8,128)(2,1)} %go_ref.3, bf16[512,1024]{1,0:T(8,128)(2,1)} %get-tuple-element.57.gofar_ref, ...), custom_call_target="tpu_custom_call" | custom-call | flops 13287555072 | bytes 41943040 | tf_op jit(solution)/shard_map/feed_forward/pallas_call | solution.py:498
  96.6 82.4 %backward.1 = (f32[512,1024]{1,0:T(8,128)}, bf16[512,1024]{1,0:T(8,128)(2,1)}, f32[16,128]{1,0:T(8,128)}, f32[128,256]{1,0:T(8,128)}, f32[128,256]{1,0:T(8,128)}...) custom-call(bf16[512,1024]{1,0:T(8,128)(2,1)} %get-tuple-element.62., ...), custom_call_target="tpu_custom_call" | custom-call | flops 16106127360 | bytes 62914560 | tf_op jit(solution)/shard_map/backward/pallas_call | solution.py:915
  179.0 5.2 %results.1 = (bf16[512,1024]{1,0:T(8,128)(2,1)}, f32[512,1024]{1,0:T(8,128)}, f32[32]{0:T(128)}, f32[32]{0:T(128)}, f32[4,4]{1,0:T(4,128)}, /*index=5*/f32[4,4]{...) custom-call(f32[512,1024]{1,0:T(8,128)} %get-tuple-element.55.middle, ...), custom_call_target="tpu_custom_call" | custom-call | tf_op jit(solution)/shard_map/results/pallas_call | solution.py:999

commit v5 on v4

--- a/solution.py
+++ b/solution.py
@@ -819,8 +819,8 @@
     plan[7].append(input_gradient)
     plan[8].append(functools.partial(far_stage, 1))
     plan[8].append(xf_last[0].start)
-    plan[12].extend(functools.partial(side_stage, 0, r) for r in order)
-    plan[15].extend(functools.partial(rank_stage, 0, r) for r in range(ranks - 2, 0, -2))
+    plan[10].extend(functools.partial(side_stage, 0, r) for r in order)
+    plan[11].extend(functools.partial(rank_stage, 0, r) for r in range(ranks - 2, 0, -2))
     for k in range(steps):
 
         @pl.when(u == k)
@@ -896,7 +896,7 @@
             copy.wait_send()
 
 
-def backward(wide, buckets, ff, ga, x, gain, gain2, fsum, gm, e, ids, out, wo_all, ctx, linv, qkv, w_all, trows=64):
+def backward(wide, buckets, ff, ga, x, gain, gain2, fsum, gm, e, ids, out, wo_all, ctx, linv, qkv, w_all, trows=128):
     slots, d = x.shape
     heads = 4
     pw = 2 * HEAD_DIM

time: 185 us -> 185 us (level)
  no operation moved by 1% of the time
where the time goes in v5:
time: 185 us; the launch traced here: 184 us
  Pallas kernels  184 us (99%)
    pallas_call x1, Pallas kernels, backward(): pl.pallas_call(functools.partial(backward_kernel, wide, heads, buckets, t...  82.4 us
    pallas_call x1, Pallas kernels, feed_forward(): pl.pallas_call(functools.partial(ffn_kernel, block, ff), in_specs=[anywhe...  51 us
    pallas_call x1, Pallas kernels, forward(): pl.pallas_call(functools.partial(forward_kernel, heads, buckets, chunk),...  44.9 us
    pallas_call x1, Pallas kernels, results(): pl.pallas_call(functools.partial(results_kernel, wide, narrow, buckets, h...  5.22 us

profile of v5, /device:TPU:0, one launch (start us, length us, event | category | flops | bytes accessed | tf_op | source)
XLA Modules:
  0.0 184.4 jit_solution(14179732286533992331)
XLA Ops:
  0.6 44.9 %forward.1 = (bf16[3,512,1024]{2,1,0:T(8,128)(2,1)}, bf16[8,2,512,512]{3,2,1,0:T(8,128)(2,1)}, bf16[512,1024]{1,0:T(8,128)(2,1)}, f32[512,1024]{1,0:T(8,128)}, b...) custom-call(s32[4]{0:T(128)} %counts_ref.1, ...), custom_call_target="tpu_custom_call" | custom-call | flops 10737418240 | bytes 41943040 | tf_op jit(solution)/shard_map/forward/pallas_call | solution.py:290
  45.6 51.0 %feed_forward.1 = (bf16[1024,1024]{1,0:T(8,128)(2,1)}, bf16[1024,2176]{1,0:T(8,128)(2,1)}, f32[512,1024]{1,0:T(8,128)}, bf16[512,1024]{1,0:T(8,128)(2,1)}, f32[1,1024]{1,0:T(1,128)}) custom-call(bf16[512,1024]{1,0:T(8,128)(2,1)} %get-tuple-element.56.x_ref, bf16[512,1024]{1,0:T(8,128)(2,1)} %go_ref.3, bf16[512,1024]{1,0:T(8,128)(2,1)} %get-tuple-element.57.gofar_ref, ...), custom_call_target="tpu_custom_call" | custom-call | flops 13287555072 | bytes 41943040 | tf_op jit(solution)/shard_map/feed_forward/pallas_call | solution.py:498
  96.6 82.4 %backward.1 = (f32[512,1024]{1,0:T(8,128)}, bf16[512,1024]{1,0:T(8,128)(2,1)}, f32[16,128]{1,0:T(8,128)}, f32[128,256]{1,0:T(8,128)}, f32[128,256]{1,0:T(8,128)}...) custom-call(bf16[512,1024]{1,0:T(8,128)(2,1)} %get-tuple-element.62., ...), custom_call_target="tpu_custom_call" | custom-call | flops 16106127360 | bytes 62914560 | tf_op jit(solution)/shard_map/backward/pallas_call | solution.py:915
  179.0 5.2 %results.1 = (bf16[512,1024]{1,0:T(8,128)(2,1)}, f32[512,1024]{1,0:T(8,128)}, f32[32]{0:T(128)}, f32[32]{0:T(128)}, f32[4,4]{1,0:T(4,128)}, /*index=5*/f32[4,4]{...) custom-call(f32[512,1024]{1,0:T(8,128)} %get-tuple-element.55.middle, ...), custom_call_target="tpu_custom_call" | custom-call | tf_op jit(solution)/shard_map/results/pallas_call | solution.py:999
